TPU v7x, 32 devices: a whole 2x2x4 slice. The times are simulated.
32 devices in a mesh: dp: 4 (over z), mp: 8 (over y, x, core).
Axes of the slice: x: 2, y: 2, z: 4, core: 2. Of those that a mesh axis runs over, the one named last changes fastest.
Arguments:
- tokens: bfloat16 [32768, 1024], P(('dp', 'mp')), may hold values from -6 to 6
- segment_ids: int32 [32, 1024], P(('dp', 'mp')), may hold values from 0 to 7, never falling along the last dimension, each value on 1 to 512 neighbouring positions
- pad_mask: int32 [32, 1024], P(('dp', 'mp')), may hold values 0 or 1
- cotangent: bfloat16 [32768, 1024], P(('dp', 'mp')), may hold values from -6 to 6
- w_query: bfloat16 [1024, 1024], replicated, may hold values from -0.1875 to 0.1875
- w_key: bfloat16 [1024, 1024], replicated, may hold values from -0.1875 to 0.1875
- w_value: bfloat16 [1024, 1024], replicated, may hold values from -0.1875 to 0.1875
- w_out: bfloat16 [1024, 1024], replicated, may hold values from -1 to 1
- w_in: bfloat16 [1024, 4096], P(None, 'mp'), may hold values from -0.1875 to 0.1875
- w_back: bfloat16 [4096, 1024], P('mp'), may hold values from -0.125 to 0.125
- params_main: float32 [8, 1024], replicated, as said below
- params_hidden: float32 [4096], P('mp'), may hold values from -3 to 3
- first_main: float32 [8, 1024], replicated, may hold values from -10 to 10
- second_main: float32 [8, 1024], replicated, may hold values from 3.2768 to 13.1072
- first_hidden: float32 [4096], P('mp'), may hold values from -10 to 10
- second_hidden: float32 [4096], P('mp'), may hold values from 3.2768 to 13.1072
- average_main: float32 [8, 1024], replicated, as said below
- average_hidden: float32 [4096], P('mp'), may hold values from -3 to 3
Outputs:
- activations: float32 [32768, 1024], P(('dp', 'mp'))
- input_grad: float32 [32768, 1024], P(('dp', 'mp'))
- grad_norm: float32 [], replicated
- grads_main: float32 [8, 1024], replicated
- grads_hidden: float32 [4096], P('mp')
- first_main_new: float32 [8, 1024], replicated
- second_main_new: float32 [8, 1024], replicated
- first_hidden_new: float32 [4096], P('mp')
- second_hidden_new: float32 [4096], P('mp')
- params_main_new: float32 [8, 1024], replicated
- params_hidden_new: float32 [4096], P('mp')
- copy_main: bfloat16 [8, 1024], replicated
- copy_hidden: bfloat16 [4096], P('mp')
- average_main_new: float32 [8, 1024], replicated
- average_hidden_new: float32 [4096], P('mp')
Inputs may be any that keep to these rules, and one draw needn't show every extreme that they name: `segment_ids`: each row is one packed sequence; its segment numbers never fall along the row and it holds 8 segments. `params_main`: rows 3 and 6 are gains near 1, the others biases of both signs. `average_main`: rows 3 and 6 are gains near 1, the others biases of both signs.
All inputs are finite; a program needn't handle non-finite values. No bound on the sum of `pad_mask` on one device may be relied on, other than what follows from the above.
Results may differ from a plain program's by a relative error of at most 0.017.
Values may be sent and summed in bfloat16 or wider, within the bound.
No kernel may reach another device: no remote copies, remote signals or barrier semaphores. Data moves between devices by JAX's collectives and lax.ppermute only.
A program may use at most 320 MiB of HBM per device.

v0:
```python
import math

import jax
import jax.numpy as jnp
from jax import lax
from jax.sharding import PartitionSpec as P

D = 1024
HEADS = 16
HEAD = 64
QBLOCK = 512
STEP = 5


def product(left, right):
    return jnp.dot(left, right, preferred_element_type=jnp.float32)


def normed(resid):
    center = resid - jnp.mean(resid, axis=-1, keepdims=True)
    factor = lax.rsqrt(jnp.mean(center * center, axis=-1, keepdims=True) + 1e-05)
    return (center * factor, factor)


def norm_back(normal, factor, dnorm):
    return factor * (
        dnorm
        - jnp.mean(dnorm, axis=-1, keepdims=True)
        - normal * jnp.mean(dnorm * normal, axis=-1, keepdims=True)
    )


def adam_step(grad, first, second, param, average):
    first_new = 0.5 * first + 0.5 * grad
    second_new = 0.5 * second + 0.5 * grad * grad
    corr = 1.0 - 0.5**STEP
    param_new = param - 0.25 * (
        first_new / corr / (jnp.sqrt(second_new / corr) + 1e-08) + 0.01 * param
    )
    return (
        first_new,
        second_new,
        param_new,
        param_new.astype(jnp.bfloat16),
        0.8 * average + 0.2 * param_new,
    )


def gelu_exact(value):
    return jax.nn.gelu(value, approximate=False)


def on_device(
    tokens,
    segment_ids,
    pad_mask,
    cotangent,
    w_query,
    w_key,
    w_value,
    w_out,
    w_in,
    w_back,
    params_main,
    params_hidden,
    first_main,
    second_main,
    first_hidden,
    second_hidden,
    average_main,
    average_hidden,
):
    rows_all = tokens.shape[0]
    seqs = segment_ids.shape[0]
    length = segment_ids.shape[1]
    block = QBLOCK
    nblock = length // block
    positions = jnp.arange(length)
    width = params_hidden.shape[0]
    total_hidden = width * lax.axis_size("mp")
    query = (product(tokens, w_query) + params_main[0]).astype(jnp.bfloat16)
    keys = product(tokens, w_key).astype(jnp.bfloat16)
    values = (product(tokens, w_value) + params_main[1]).astype(jnp.bfloat16)
    q_blocks = query.reshape(seqs, nblock, block, HEADS, HEAD)
    k_seqs = keys.reshape(seqs, length, HEADS, HEAD)
    v_seqs = values.reshape(seqs, length, HEADS, HEAD)

    def visible(seg_row, pad_row, index):
        seg_query = lax.dynamic_slice_in_dim(seg_row, index * block, block)
        query_pos = index * block + jnp.arange(block)
        return (seg_query[:, None] == seg_row[None, :]) & (
            (pad_row[None, :] == 1) | (query_pos[:, None] == positions[None, :])
        )

    def scores_of(q_blk, k_seq, vis):
        scores = (
            jnp.einsum("qhd,khd->hqk", q_blk, k_seq, preferred_element_type=jnp.float32) * 0.125
        )
        return jnp.where(vis[None], scores, -1000000000.0)

    def attend_seq(args):
        q_seq, k_seq, v_seq, seg_row, pad_row = args

        def one_block(index):
            scores = scores_of(q_seq[index], k_seq, visible(seg_row, pad_row, index))
            top = jnp.max(scores, axis=-1, keepdims=True)
            expd = jnp.exp(scores - top)
            total = jnp.sum(expd, axis=-1, keepdims=True)
            probs = (expd / total).astype(jnp.bfloat16)
            mixed = jnp.einsum("hqk,khd->qhd", probs, v_seq, preferred_element_type=jnp.float32)
            return (mixed, (top + jnp.log(total))[..., 0])

        return lax.map(one_block, jnp.arange(nblock))

    mixed, lse = lax.map(attend_seq, (q_blocks, k_seqs, v_seqs, segment_ids, pad_mask))
    mixed_low = mixed.reshape(rows_all, D).astype(jnp.bfloat16)
    resid_one = tokens.astype(jnp.float32) + product(mixed_low, w_out) + params_main[2]
    normal_one, factor_one = normed(resid_one)
    hidden_in = normal_one * params_main[3] + params_main[4]
    hidden_low = hidden_in.astype(jnp.bfloat16)
    dy = cotangent.astype(jnp.float32) * pad_mask.reshape(rows_all)[:, None].astype(jnp.float32)
    zeta = product(lax.all_gather(hidden_low, "mp", axis=0, tiled=True), w_in) + params_hidden
    upper, gelu_pull = jax.vjp(gelu_exact, zeta)
    upper_low = upper.astype(jnp.bfloat16)
    ffn = (
        lax.psum_scatter(
            product(upper_low, w_back).astype(jnp.bfloat16), "mp", scatter_dimension=0, tiled=True
        ).astype(jnp.float32)
        + params_main[5]
    )
    normal_two, factor_two = normed(hidden_in + ffn)
    dresid_two = norm_back(normal_two, factor_two, dy * params_main[6])
    dupper = product(
        lax.all_gather(dresid_two.astype(jnp.bfloat16), "mp", axis=0, tiled=True), w_back.T
    )
    dzeta = gelu_pull(dupper)[0]
    dzeta_low = dzeta.astype(jnp.bfloat16)
    dhidden = dresid_two + lax.psum_scatter(
        product(dzeta_low, w_in.T).astype(jnp.bfloat16), "mp", scatter_dimension=0, tiled=True
    ).astype(jnp.float32)
    hidden_vec = lax.dynamic_update_slice_in_dim(
        jnp.zeros((total_hidden,), jnp.float32),
        jnp.sum(dzeta, axis=0),
        lax.axis_index("mp") * width,
        0,
    )
    activations = normal_two * params_main[6] + params_main[7]
    grad_gain_two = jnp.sum(dy * normal_two, axis=0)
    grad_shift_two = jnp.sum(dy, axis=0)
    grad_bias_two = jnp.sum(dresid_two, axis=0)
    grad_gain_one = jnp.sum(dhidden * normal_one, axis=0)
    grad_shift_one = jnp.sum(dhidden, axis=0)
    dresid_one = norm_back(normal_one, factor_one, dhidden * params_main[3])
    grad_bias_out = jnp.sum(dresid_one, axis=0)
    dmixed = product(dresid_one.astype(jnp.bfloat16), w_out.T).astype(jnp.bfloat16)
    d_blocks = dmixed.reshape(seqs, nblock, block, HEADS, HEAD)

    def back_seq(args):
        q_seq, k_seq, v_seq, d_seq, l_seq, seg_row, pad_row = args

        def one_step(carry, index):
            dkeys, dvalues = carry
            q_blk = q_seq[index]
            d_blk = d_seq[index]
            scores = scores_of(q_blk, k_seq, visible(seg_row, pad_row, index))
            probs = jnp.exp(scores - l_seq[index][..., None])
            dprobs = jnp.einsum("qhd,khd->hqk", d_blk, v_seq, preferred_element_type=jnp.float32)
            delta = jnp.sum(probs * dprobs, axis=-1, keepdims=True)
            dscores = (probs * (dprobs - delta)).astype(jnp.bfloat16)
            dquery = 0.125 * jnp.einsum(
                "hqk,khd->qhd", dscores, k_seq, preferred_element_type=jnp.float32
            )
            dkeys = dkeys + 0.125 * jnp.einsum(
                "hqk,qhd->khd", dscores, q_blk, preferred_element_type=jnp.float32
            )
            dvalues = dvalues + jnp.einsum(
                "hqk,qhd->khd",
                probs.astype(jnp.bfloat16),
                d_blk,
                preferred_element_type=jnp.float32,
            )
            return ((dkeys, dvalues), dquery)

        empty = jnp.zeros((length, HEADS, HEAD), jnp.float32)
        (dkeys, dvalues), dquery = lax.scan(one_step, (empty, empty), jnp.arange(nblock))
        return (dquery, dkeys, dvalues)

    dquery, dkeys, dvalues = lax.map(
        back_seq, (q_blocks, k_seqs, v_seqs, d_blocks, lse, segment_ids, pad_mask)
    )
    dquery = dquery.reshape(rows_all, D)
    dkeys = dkeys.reshape(rows_all, D)
    dvalues = dvalues.reshape(rows_all, D)
    input_grad = dresid_one + product(dquery.astype(jnp.bfloat16), w_query.T)
    input_grad = input_grad + product(dkeys.astype(jnp.bfloat16), w_key.T)
    input_grad = input_grad + product(dvalues.astype(jnp.bfloat16), w_value.T)
    local_main = jnp.stack(
        [
            jnp.sum(dquery, axis=0),
            jnp.sum(dvalues, axis=0),
            grad_bias_out,
            grad_gain_one,
            grad_shift_one,
            grad_bias_two,
            grad_gain_two,
            grad_shift_two,
        ]
    )
    grad_main, hidden_total = lax.psum((local_main, hidden_vec), ("dp", "mp"))
    grad_hid = lax.dynamic_slice_in_dim(hidden_total, lax.axis_index("mp") * width, width, 0)
    grad_norm = jnp.sqrt(jnp.sum(grad_main * grad_main) + jnp.sum(hidden_total * hidden_total))
    tokens_all = rows_all * lax.axis_size("dp") * lax.axis_size("mp")
    limit = 0.01 * math.sqrt(tokens_all * (8 * D + total_hidden))
    scale_factor = jnp.minimum(1.0, limit / (grad_norm + 1e-06))
    grad_main = grad_main * scale_factor
    grad_hid = grad_hid * scale_factor
    fm, sm, pm, cm, am = adam_step(grad_main, first_main, second_main, params_main, average_main)
    fh, sh, ph, ch, ah = adam_step(
        grad_hid, first_hidden, second_hidden, params_hidden, average_hidden
    )
    return (
        activations,
        input_grad,
        grad_norm,
        grad_main,
        grad_hid,
        fm,
        sm,
        fh,
        sh,
        pm,
        ph,
        cm,
        ch,
        am,
        ah,
    )


def solution(mesh):
    placed = (
        P(("dp", "mp"), None),
        P(("dp", "mp"), None),
        P(("dp", "mp"), None),
        P(("dp", "mp"), None),
        P(),
        P(),
        P(),
        P(),
        P(None, "mp"),
        P("mp", None),
        P(),
        P("mp"),
        P(),
        P(),
        P("mp"),
        P("mp"),
        P(),
        P("mp"),
    )
    return jax.shard_map(
        on_device,
        mesh=mesh,
        in_specs=placed,
        out_specs=(
            P(("dp", "mp"), None),
            P(("dp", "mp"), None),
            P(),
            P(),
            P("mp"),
            P(),
            P(),
            P("mp"),
            P("mp"),
            P(),
            P("mp"),
            P(),
            P("mp"),
            P(),
            P("mp"),
        ),
        check_vma=False,
    )
```

profile of v0, /device:TPU:0, one launch (start us, length us, event | category | flops | bytes accessed | tf_op | source)
XLA Modules:
  0.0 1026.9 jit_solution(4091869219329709694)
XLA Ops:
  20.3 6.3 reshape.288
  44.0 100.1 %while.50 = (s32[]{:T(128)}, bf16[2,512,16,64]{1,3,2,0:T(8,128)(2,1)}, f32[2,16,512]{2,1,0:T(8,128)S(1)}, s32[2]{0:T(128)S(1)}, s32[1024]{0:T(1024)S(1)}, /*inde...) while((s32[]{:T(128)}, ...), condition=%wide.region_3.4_spmd.clone.clone, body=%wide.region_0.3_spmd.clone.sunk.clone | while | flops 2250237440 | bytes 118772448 | solution.py:113
  48.2 15.6 %fusion.137 = (f32[16,512]{1,0:T(8,128)S(1)}, f32[16,512,1024]{2,1,0:T(8,128)}) fusion(pred[512,1024]{1,0:T(8,128)(4,1)S(1)} %fusion.136, bf16[1024,16,64]{0,2,1:T(8,128)(2,1)} %get-tuple-element.653, bf16[2,512,16,64]{1,3,2,0:T(8,128)(2,1)} %get-tuple-element.652, s32[]{:T(128)S(6)} %select_n.78), kind=kOutput, calls=%fused_computation.5.clone.1.clone | convolution fusion | flops 1098899456 | bytes 37257220 | tf_op jit(solution)/shard_map/while/body/eval_jaxpr/while/body/eval_jaxpr/qhd,khd->hqk/dot_general | solution.py:97
  63.8 15.0 %fusion.138 = f32[16,512]{1,0:T(8,128)S(1)} fusion(f32[16,512,1024]{2,1,0:T(8,128)} %get-tuple-element.580, f32[16,512]{1,0:T(8,128)S(1)} %get-tuple-element.581, pred[512,1024]{1,0:T(8,128)(4,1)S(1)} %fusion.136), kind=kLoop, calls=%fused_computation.6.clone.1.clone | loop fusion | flops 33546240 | bytes 34144256 | tf_op jit(solution)/shard_map/while/body/eval_jaxpr/while/body/eval_jaxpr/reduce_sum | solution.py:108
  78.9 15.2 %bitcast_dynamic-update-slice_fusion.9 = bf16[2,512,16,64]{1,3,2,0:T(8,128)(2,1)} fusion(bf16[2,512,16,64]{1,3,2,0:T(8,128)(2,1)} %get-tuple-element.638, s32[]{:T(128)} %get-tuple-element.637, bf16[1024,16,64]{0,2,1:T(8,128)(2,1)S(1)} %copy-done.4, f32[16,512,1024]{2,1,0:T(8,128)} %get-tuple-element.580, f32[16,512]{1,0:T(8,128)S(1)} %fusion.138, ...), kind=kOutput, calls=%fused_computation.8.clone.1.clone | convolution fusion | flops 1115684864 | bytes 38339072 | tf_op jit(solution)/shard_map/while/body/eval_jaxpr/while/body/eval_jaxpr/hqk,khd->qhd/dot_general | solution.py:110
  98.0 15.6 %fusion.137 = (f32[16,512]{1,0:T(8,128)S(1)}, f32[16,512,1024]{2,1,0:T(8,128)}) fusion(pred[512,1024]{1,0:T(8,128)(4,1)S(1)} %fusion.136, bf16[1024,16,64]{0,2,1:T(8,128)(2,1)} %get-tuple-element.653, bf16[2,512,16,64]{1,3,2,0:T(8,128)(2,1)} %get-tuple-element.652, s32[]{:T(128)S(6)} %select_n.78), kind=kOutput, calls=%fused_computation.5.clone.1.clone | convolution fusion | flops 1098899456 | bytes 37257220 | tf_op jit(solution)/shard_map/while/body/eval_jaxpr/while/body/eval_jaxpr/qhd,khd->hqk/dot_general | solution.py:97
  113.6 15.0 %fusion.138 = f32[16,512]{1,0:T(8,128)S(1)} fusion(f32[16,512,1024]{2,1,0:T(8,128)} %get-tuple-element.580, f32[16,512]{1,0:T(8,128)S(1)} %get-tuple-element.581, pred[512,1024]{1,0:T(8,128)(4,1)S(1)} %fusion.136), kind=kLoop, calls=%fused_computation.6.clone.1.clone | loop fusion | flops 33546240 | bytes 34144256 | tf_op jit(solution)/shard_map/while/body/eval_jaxpr/while/body/eval_jaxpr/reduce_sum | solution.py:108
  128.7 15.2 %bitcast_dynamic-update-slice_fusion.9 = bf16[2,512,16,64]{1,3,2,0:T(8,128)(2,1)} fusion(bf16[2,512,16,64]{1,3,2,0:T(8,128)(2,1)} %get-tuple-element.638, s32[]{:T(128)} %get-tuple-element.637, bf16[1024,16,64]{0,2,1:T(8,128)(2,1)S(1)} %copy-done.4, f32[16,512,1024]{2,1,0:T(8,128)} %get-tuple-element.580, f32[16,512]{1,0:T(8,128)S(1)} %fusion.138, ...), kind=kOutput, calls=%fused_computation.8.clone.1.clone | convolution fusion | flops 1115684864 | bytes 38339072 | tf_op jit(solution)/shard_map/while/body/eval_jaxpr/while/body/eval_jaxpr/hqk,khd->qhd/dot_general | solution.py:110
  155.5 92.7 %all-gather.3.cloned.1.call-done = bf16[8192,1024]{0,1:T(8,128)(2,1)} async-done(((bf16[1024,1024]{0,1:T(8,128)(2,1)}), bf16[8192,1024]{0,1:T(8,128)(2,1)}) %all-gather.3.cloned.1.call-update) | async-done | bytes 16777232 | tf_op jit(solution)/shard_map/all_gather | solution.py:122
  248.2 47.1 %fusion.39 = (f32[8192,512]{1,0:T(8,128)}, f32[8192,512]{1,0:T(8,128)}) fusion(f32[512]{0:T(512)S(1)} %copy-done.49, bf16[8192,1024]{0,1:T(8,128)(2,1)} %all-gather.3.cloned.1.call-done, bf16[1024,512]{1,0:T(8,128)(2,1)} %param.30), kind=kOutput, calls=%fused_computation.53 | convolution fusion | flops 8854175744 | bytes 51382272 | tf_op jit(solution)/shard_map/dot_general | solution.py:16
  295.3 21.4 %convolution_convert_fusion.1 = bf16[8192,1024]{0,1:T(8,128)(2,1)} fusion(bf16[512,1024]{1,0:T(8,128)(2,1)S(1)} %copy-done.56, f32[8192,512]{1,0:T(8,128)} %get-tuple-element.428, f32[8192,512]{1,0:T(8,128)} %get-tuple-element.429, f32[512]{0:T(512)S(1)} %copy-done.49), kind=kOutput, calls=%fused_computation.70 | convolution fusion | flops 8615100416 | bytes 51382272 | tf_op jit(solution)/shard_map/dot_general | solution.py:16
  321.3 111.5 %reduce-scatter.3.cloned.1.call-done = bf16[1024,1024]{0,1:T(8,128)(2,1)} async-done(((bf16[8192,1024]{0,1:T(8,128)(2,1)}), bf16[1024,1024]{0,1:T(8,128)(2,1)}) %reduce-scatter.3.cloned.1.call-update) | async-done | bytes 2097168 | tf_op jit(solution)/shard_map/reduce_scatter | solution.py:126
  445.9 90.0 %all-gather.5.cloned.1.call-done = bf16[8192,1024]{0,1:T(8,128)(2,1)} async-done(((bf16[1024,1024]{0,1:T(8,128)(2,1)}), bf16[8192,1024]{0,1:T(8,128)(2,1)}) %all-gather.5.cloned.1.call-update) | async-done | bytes 16777232 | tf_op jit(solution)/shard_map/all_gather | solution.py:134
  535.9 25.7 %fusion.63 = (f32[512]{0:T(512)S(1)}, bf16[8192,512]{1,0:T(8,128)(2,1)}) fusion(f32[8192,512]{1,0:T(8,128)} %get-tuple-element.428, f32[8192,512]{1,0:T(8,128)} %get-tuple-element.429, f32[512]{0:T(512)S(1)} %copy-done.49, bf16[8192,1024]{0,1:T(8,128)(2,1)} %all-gather.5.cloned.1.call-done, bf16[512,1024]{1,0:T(8,128)(2,1)} %param.31), kind=kOutput, calls=%fused_computation.126 | convolution fusion | flops 8657043456 | bytes 59772928 | tf_op jit(solution)/shard_map/dot_general | solution.py:16
  561.6 14.8 %convolution_convert_fusion = bf16[8192,1024]{0,1:T(8,128)(2,1)} fusion(bf16[1024,512]{1,0:T(8,128)(2,1)} %param.30, bf16[8192,512]{1,0:T(8,128)(2,1)} %get-tuple-element.402), kind=kOutput, calls=%fused_computation.69 | convolution fusion | flops 8598323200 | bytes 26214400 | tf_op jit(solution)/shard_map/dot_general | solution.py:16
  582.0 110.6 %reduce-scatter.5.cloned.1.call-done = bf16[1024,1024]{0,1:T(8,128)(2,1)} async-done(((bf16[8192,1024]{0,1:T(8,128)(2,1)}), bf16[1024,1024]{0,1:T(8,128)(2,1)}) %reduce-scatter.5.cloned.1.call-update) | async-done | bytes 2097168 | tf_op jit(solution)/shard_map/reduce_scatter | solution.py:138
  692.5 6.2 multiply_reduce_fusion.2
  708.6 6.3 reshape.287
  720.6 223.8 %while.51 = (s32[]{:T(128)}, f32[1024,16,64]{0,2,1:T(8,128)}, f32[1024,16,64]{0,2,1:T(8,128)}, f32[2,512,16,64]{1,3,2,0:T(8,128)}, s32[2]{0:T(128)S(1)}, /*index...) while((s32[]{:T(128)}, f32[1024,16,64]{0,2,1:T(8,128)}, ...), condition=%wide.region_16.17_spmd.clone.clone, body=%wide.region_14.16_spmd.clone.sunk.clone | while | flops 5502395904 | bytes 300143392 | solution.py:185
  724.6 14.6 %fusion.148 = f32[16,512,1024]{2,1,0:T(8,128)} fusion(bf16[1024,16,64]{0,2,1:T(8,128)(2,1)S(1)} %get-tuple-element.687, bf16[2,512,16,64]{1,3,2,0:T(8,128)(2,1)} %get-tuple-element.684, s32[]{:T(128)S(6)} %select_n.82), kind=kOutput, calls=%fused_computation.37.clone.1.clone | convolution fusion | flops 1073741824 | bytes 36700164 | tf_op jit(solution)/shard_map/while/body/eval_jaxpr/while/body/eval_jaxpr/qhd,khd->hqk/dot_general | solution.py:97
  739.1 25.6 %multiply_reduce_fusion.12 = (f32[16,512]{1,0:T(8,128)S(1)}, f32[16,512,1024]{2,1,0:T(8,128)}) fusion(f32[16,512,1024]{2,1,0:T(8,128)} %fusion.148, f32[16,512]{1,0:T(8,128)S(1)} %dynamic-slice_bitcast_fusion.3, pred[512,1024]{1,0:T(8,128)(4,1)S(1)} %fusion.149, bf16[1024,16,64]{0,2,1:T(8,128)(2,1)S(1)} %copy-done.5, ...), kind=kOutput, calls=%fused_computation.22.clone.1.clone | convolution fusion | flops 1115676672 | bytes 70844416 | tf_op jit(solution)/shard_map/while/body/eval_jaxpr/while/body/eval_jaxpr/qhd,khd->hqk/dot_general | solution.py:167
  764.7 27.8 %multiply_convert_fusion.5 = bf16[16,512,1024]{2,1,0:T(8,128)(2,1)} fusion(f32[16,512,1024]{2,1,0:T(8,128)} %get-tuple-element.609, f32[16,512,1024]{2,1,0:T(8,128)} %fusion.148, f32[16,512]{1,0:T(8,128)S(1)} %get-tuple-element.610, f32[16,512]{1,0:T(8,128)S(1)} %dynamic-slice_bitcast_fusion.3, pred[512,1024]{1,0:T(8,128)(4,1)S(1)} %fusion.149), kind=kLoop, calls=%fused_computation.21.clone.1.clone | loop fusion | flops 50331648 | bytes 84475904 | tf_op jit(solution)/shard_map/while/body/eval_jaxpr/while/body/eval_jaxpr/convert_element_type | solution.py:169
  792.5 11.1 %bitcast_add_fusion.6 = f32[1024,16,64]{0,2,1:T(8,128)} fusion(f32[1024,16,64]{0,2,1:T(8,128)} %get-tuple-element.668, bf16[16,512,1024]{2,1,0:T(8,128)(2,1)} %multiply_convert_fusion.5, pred[]{:T(512)S(6)} %compare.4, bf16[2,512,16,64]{1,3,2,0:T(8,128)(2,1)} %get-tuple-element.684, s32[]{:T(128)S(6)} %select_n.82), kind=kOutput, calls=%fused_computation.28.clone.1.clone | convolution fusion | flops 1076887552 | bytes 26214404 | tf_op jit(solution)/shard_map/while/body/eval_jaxpr/while/body/eval_jaxpr/hqk,qhd->khd/dot_general | solution.py:173
  803.6 10.2 bitcast_dynamic-update-slice_fusion.11
  813.7 17.5 %bitcast_add_fusion.7 = f32[1024,16,64]{0,2,1:T(8,128)} fusion(f32[1024,16,64]{0,2,1:T(8,128)} %get-tuple-element.669, f32[16,512,1024]{2,1,0:T(8,128)} %fusion.148, f32[16,512]{1,0:T(8,128)S(1)} %dynamic-slice_bitcast_fusion.3, pred[512,1024]{1,0:T(8,128)(4,1)S(1)} %fusion.149, pred[]{:T(512)S(6)} %compare.4, ...), kind=kOutput, calls=%fused_computation.27.clone.1.clone | convolution fusion | flops 1109393408 | bytes 43548676 | tf_op jit(solution)/shard_map/while/body/eval_jaxpr/while/body/eval_jaxpr/hqk,qhd->khd/dot_general | solution.py:176
  835.2 14.6 %fusion.148 = f32[16,512,1024]{2,1,0:T(8,128)} fusion(bf16[1024,16,64]{0,2,1:T(8,128)(2,1)S(1)} %get-tuple-element.687, bf16[2,512,16,64]{1,3,2,0:T(8,128)(2,1)} %get-tuple-element.684, s32[]{:T(128)S(6)} %select_n.82), kind=kOutput, calls=%fused_computation.37.clone.1.clone | convolution fusion | flops 1073741824 | bytes 36700164 | tf_op jit(solution)/shard_map/while/body/eval_jaxpr/while/body/eval_jaxpr/qhd,khd->hqk/dot_general | solution.py:97
  849.8 25.6 %multiply_reduce_fusion.12 = (f32[16,512]{1,0:T(8,128)S(1)}, f32[16,512,1024]{2,1,0:T(8,128)}) fusion(f32[16,512,1024]{2,1,0:T(8,128)} %fusion.148, f32[16,512]{1,0:T(8,128)S(1)} %dynamic-slice_bitcast_fusion.3, pred[512,1024]{1,0:T(8,128)(4,1)S(1)} %fusion.149, bf16[1024,16,64]{0,2,1:T(8,128)(2,1)S(1)} %copy-done.5, ...), kind=kOutput, calls=%fused_computation.22.clone.1.clone | convolution fusion | flops 1115676672 | bytes 70844416 | tf_op jit(solution)/shard_map/while/body/eval_jaxpr/while/body/eval_jaxpr/qhd,khd->hqk/dot_general | solution.py:167
  875.3 27.8 %multiply_convert_fusion.5 = bf16[16,512,1024]{2,1,0:T(8,128)(2,1)} fusion(f32[16,512,1024]{2,1,0:T(8,128)} %get-tuple-element.609, f32[16,512,1024]{2,1,0:T(8,128)} %fusion.148, f32[16,512]{1,0:T(8,128)S(1)} %get-tuple-element.610, f32[16,512]{1,0:T(8,128)S(1)} %dynamic-slice_bitcast_fusion.3, pred[512,1024]{1,0:T(8,128)(4,1)S(1)} %fusion.149), kind=kLoop, calls=%fused_computation.21.clone.1.clone | loop fusion | flops 50331648 | bytes 84475904 | tf_op jit(solution)/shard_map/while/body/eval_jaxpr/while/body/eval_jaxpr/convert_element_type | solution.py:169
  903.1 12.3 %bitcast_add_fusion.6 = f32[1024,16,64]{0,2,1:T(8,128)} fusion(f32[1024,16,64]{0,2,1:T(8,128)} %get-tuple-element.668, bf16[16,512,1024]{2,1,0:T(8,128)(2,1)} %multiply_convert_fusion.5, pred[]{:T(512)S(6)} %compare.4, bf16[2,512,16,64]{1,3,2,0:T(8,128)(2,1)} %get-tuple-element.684, s32[]{:T(128)S(6)} %select_n.82), kind=kOutput, calls=%fused_computation.28.clone.1.clone | convolution fusion | flops 1076887552 | bytes 26214404 | tf_op jit(solution)/shard_map/while/body/eval_jaxpr/while/body/eval_jaxpr/hqk,qhd->khd/dot_general | solution.py:173
  915.4 10.1 bitcast_dynamic-update-slice_fusion.11
  925.5 18.7 %bitcast_add_fusion.7 = f32[1024,16,64]{0,2,1:T(8,128)} fusion(f32[1024,16,64]{0,2,1:T(8,128)} %get-tuple-element.669, f32[16,512,1024]{2,1,0:T(8,128)} %fusion.148, f32[16,512]{1,0:T(8,128)S(1)} %dynamic-slice_bitcast_fusion.3, pred[512,1024]{1,0:T(8,128)(4,1)S(1)} %fusion.149, pred[]{:T(512)S(6)} %compare.4, ...), kind=kOutput, calls=%fused_computation.27.clone.1.clone | convolution fusion | flops 1109393408 | bytes 43548676 | tf_op jit(solution)/shard_map/while/body/eval_jaxpr/while/body/eval_jaxpr/hqk,qhd->khd/dot_general | solution.py:176
  954.1 39.8 %all-reduce = (f32[8,1024]{1,0:T(8,128)S(1)}, f32[4096]{0:T(1024)S(1)}) all-reduce(f32[8,1024]{1,0:T(8,128)S(1)} %stack.35, f32[4096]{0:T(1024)S(1)} %copy-done.32), channel_id=1, replica_groups=mesh['dp'=4,'mp'=8] {'dp','mp'}, use_global_device_ids=true, to_apply=%region_25.26 | all-reduce | flops 12288 | bytes 98304 | tf_op jit(solution)/shard_map/psum | solution.py:209
  (207 shorter events, 118.9 us)
Async XLA Ops:
  7.2 141.5 %copy-start = (bf16[1024,1024]{1,0:T(8,128)(2,1)S(1)}, bf16[1024,1024]{1,0:T(8,128)(2,1)}, u32[]{:S(2)}) copy-start(bf16[1024,1024]{1,0:T(8,128)(2,1)} %param.29) | copy-start | bytes 6291460
  7.2 241.0 %all-gather.3.cloned.1.call-start = ((), (), s32[]{:S(2)}) async-start(), calls=%async_computation.2 | async-start | bytes 18874368 | tf_op jit(solution)/shard_map/all_gather | solution.py:122
  38.0 6.0 copy-start.19
  63.8 15.1 %copy-start.4 = (bf16[1024,16,64]{0,2,1:T(8,128)(2,1)S(1)}, bf16[1024,16,64]{0,2,1:T(8,128)(2,1)}, u32[]{:S(2)}) copy-start(bf16[1024,16,64]{0,2,1:T(8,128)(2,1)} %get-tuple-element.654) | copy-start | bytes 6291460 | tf_op jit(solution)/shard_map/while/body/eval_jaxpr/while
  113.6 15.1 %copy-start.4 = (bf16[1024,16,64]{0,2,1:T(8,128)(2,1)S(1)}, bf16[1024,16,64]{0,2,1:T(8,128)(2,1)}, u32[]{:S(2)}) copy-start(bf16[1024,16,64]{0,2,1:T(8,128)(2,1)} %get-tuple-element.654) | copy-start | bytes 6291460 | tf_op jit(solution)/shard_map/while/body/eval_jaxpr/while
  153.4 94.7 %copy-start.49 = (f32[512]{0:T(512)S(1)}, f32[512]{0:T(512)}, u32[]{:S(2)}) copy-start(f32[512]{0:T(512)} %param.33) | copy-start | bytes 6148
  155.4 139.8 %copy-start.56 = (bf16[512,1024]{1,0:T(8,128)(2,1)S(1)}, bf16[512,1024]{1,0:T(8,128)(2,1)}, u32[]{:S(2)}) copy-start(bf16[512,1024]{1,0:T(8,128)(2,1)} %param.31) | copy-start | bytes 3145732
  155.5 277.3 %reduce-scatter.3.cloned.1.call-start = ((), (), s32[]{:S(2)}) async-start(), calls=%async_computation.3 | async-start | bytes 18874368 | tf_op jit(solution)/shard_map/reduce_scatter | solution.py:126
  316.7 116.1 %copy-start.24 = (f32[1024]{0:T(1024)S(1)}, f32[1024]{0:T(1024)}, u32[]{:S(2)}) copy-start(f32[1024]{0:T(1024)} %copy-done.23) | copy-start | bytes 12292
  316.7 116.1 %copy-start.28 = (f32[1,1024]{1,0:T(1,128)S(1)}, f32[1,1024]{1,0:T(1,128)}, u32[]{:S(2)}) copy-start(f32[1,1024]{1,0:T(1,128)} %get-tuple-element.421) | copy-start | bytes 12292
  316.7 116.1 %copy-start.30 = (f32[1024]{0:T(1024)S(1)}, f32[1024]{0:T(1024)}, u32[]{:S(2)}) copy-start(f32[1024]{0:T(1024)} %copy-done.29) | copy-start | bytes 12292
  316.7 116.1 %copy-start.35 = (f32[1,1024]{1,0:T(1,128)S(1)}, f32[1,1024]{1,0:T(1,128)}, u32[]{:S(2)}) copy-start(f32[1,1024]{1,0:T(1,128)} %get-tuple-element.420) | copy-start | bytes 12292
  316.7 116.1 %copy-start.45 = (f32[1,1024]{1,0:T(1,128)S(1)}, f32[1,1024]{1,0:T(1,128)}, u32[]{:S(2)}) copy-start(f32[1,1024]{1,0:T(1,128)} %get-tuple-element.419) | copy-start | bytes 12292
  316.7 219.1 %all-gather.5.cloned.1.call-start = ((), (), s32[]{:S(2)}) async-start(), calls=%async_computation.4 | async-start | bytes 18874368 | tf_op jit(solution)/shard_map/all_gather | solution.py:134
  445.8 246.7 %reduce-scatter.5.cloned.1.call-start = ((), (), s32[]{:S(2)}) async-start(), calls=%async_computation.5 | async-start | bytes 18874368 | tf_op jit(solution)/shard_map/reduce_scatter | solution.py:138
  582.0 116.7 %copy-start.31 = (f32[4096]{0:T(1024)}, f32[4096]{0:T(1024)S(1)}, u32[]{:S(2)}) copy-start(f32[4096]{0:T(1024)S(1)} %dynamic_update_slice.27) | copy-start | bytes 49156
  692.5 6.2 copy-start.7
  692.5 6.5 copy-start.8
  692.5 7.1 copy-start.14
  724.5 14.6 %copy-start.5 = (bf16[1024,16,64]{0,2,1:T(8,128)(2,1)S(1)}, bf16[1024,16,64]{0,2,1:T(8,128)(2,1)}, u32[]{:S(2)}) copy-start(bf16[1024,16,64]{0,2,1:T(8,128)(2,1)} %get-tuple-element.690) | copy-start | bytes 6291460 | tf_op jit(solution)/shard_map/while/body/eval_jaxpr/while
  724.5 14.6 %copy-start.11 = (bf16[2,512,16,64]{1,3,2,0:T(8,128)(2,1)S(1)}, bf16[2,512,16,64]{1,3,2,0:T(8,128)(2,1)}, u32[]{:S(2)}) copy-start(bf16[2,512,16,64]{1,3,2,0:T(8,128)(2,1)} %get-tuple-element.689) | copy-start | bytes 6291460 | tf_op jit(solution)/shard_map/while/body/eval_jaxpr/while
  835.2 14.6 %copy-start.5 = (bf16[1024,16,64]{0,2,1:T(8,128)(2,1)S(1)}, bf16[1024,16,64]{0,2,1:T(8,128)(2,1)}, u32[]{:S(2)}) copy-start(bf16[1024,16,64]{0,2,1:T(8,128)(2,1)} %get-tuple-element.690) | copy-start | bytes 6291460 | tf_op jit(solution)/shard_map/while/body/eval_jaxpr/while
  835.2 14.6 %copy-start.11 = (bf16[2,512,16,64]{1,3,2,0:T(8,128)(2,1)S(1)}, bf16[2,512,16,64]{1,3,2,0:T(8,128)(2,1)}, u32[]{:S(2)}) copy-start(bf16[2,512,16,64]{1,3,2,0:T(8,128)(2,1)} %get-tuple-element.689) | copy-start | bytes 6291460 | tf_op jit(solution)/shard_map/while/body/eval_jaxpr/while
  948.5 48.0 %copy-start.25 = (f32[8,1024]{1,0:T(8,128)S(1)}, f32[8,1024]{1,0:T(8,128)}, u32[]{:S(2)}) copy-start(f32[8,1024]{1,0:T(8,128)} %param.32) | copy-start | bytes 98308
  948.5 48.0 %copy-start.36 = (f32[8,1024]{1,0:T(8,128)S(1)}, f32[8,1024]{1,0:T(8,128)}, u32[]{:S(2)}) copy-start(f32[8,1024]{1,0:T(8,128)} %param.38) | copy-start | bytes 98308
  948.5 48.0 %copy-start.37 = (f32[8,1024]{1,0:T(8,128)S(1)}, f32[8,1024]{1,0:T(8,128)}, u32[]{:S(2)}) copy-start(f32[8,1024]{1,0:T(8,128)} %param.35) | copy-start | bytes 98308
  948.5 48.0 %copy-start.38 = (f32[8,1024]{1,0:T(8,128)S(1)}, f32[8,1024]{1,0:T(8,128)}, u32[]{:S(2)}) copy-start(f32[8,1024]{1,0:T(8,128)} %param.34) | copy-start | bytes 98308
  948.5 49.3 %copy-start.50 = (f32[512]{0:T(512)S(1)}, f32[512]{0:T(512)}, u32[]{:S(2)}) copy-start(f32[512]{0:T(512)} %param.33) | copy-start | bytes 6148
  948.5 49.3 %copy-start.51 = (f32[512]{0:T(512)S(1)}, f32[512]{0:T(512)}, u32[]{:S(2)}) copy-start(f32[512]{0:T(512)} %param.39) | copy-start | bytes 6148
  948.5 49.3 %copy-start.52 = (f32[512]{0:T(512)S(1)}, f32[512]{0:T(512)}, u32[]{:S(2)}) copy-start(f32[512]{0:T(512)} %param.37) | copy-start | bytes 6148
  948.5 49.3 %copy-start.53 = (f32[512]{0:T(512)S(1)}, f32[512]{0:T(512)}, u32[]{:S(2)}) copy-start(f32[512]{0:T(512)} %param.36) | copy-start | bytes 6148
  1009.3 9.7 copy-start.1
  (32 other events, 118.5 us)
Sparse Core Ops, SparseCore 0:
  155.6 92.5 all-gather.2
  316.8 115.9 reduce-scatter.2
  446.0 89.8 all-gather.4
  576.5 115.9 reduce-scatter.4
where the time goes:
time: 1030 us
  waiting for transfers between devices  405 us (39%)
  matrix products  364 us (35%)
  other arithmetic  127 us (12%)
  local copies, waits for them, and re-layouts  62.8 us (6%)
  blocking collectives  39.8 us (4%)
  between operations  17.1 us (2%)
  loops' own time  11.1 us (1%)
    dot_general x12, matrix products, product(): return jnp.dot(left, right, preferred_element_type=jnp.float32)  142 us
    reduce_scatter x1, waiting for transfers between devices, on_device(): lax.psum_scatter(product(upper_low, w_back).astype(jnp.bfloat16), 'mp', s...  112 us
    reduce_scatter x1, waiting for transfers between devices, on_device(): lax.psum_scatter(product(dzeta_low, w_in.T).astype(jnp.bfloat16), 'mp', s...  111 us
    all_gather x1, waiting for transfers between devices, on_device(): lax.all_gather(hidden_low, 'mp', axis=0, tiled=True)  92.7 us
    all_gather x1, waiting for transfers between devices, on_device(): lax.all_gather(dresid_two.astype(jnp.bfloat16), 'mp', axis=0, tiled=True)  90 us
    dot_general x4, matrix products, scores_of(): jnp.einsum('qhd,khd->hqk', q_blk, k_seq, preferred_element_type=jnp.float32)  60.3 us
    convert_element_type x2, other arithmetic, one_step(): dscores = (probs * (dprobs - delta)).astype(jnp.bfloat16)  55.5 us
    dot_general x2, matrix products, one_step(): jnp.einsum('qhd,khd->hqk', d_blk, v_seq, preferred_element_type=jnp.float32)  51.2 us
  transfers between devices with their start and end apart: 4, of which 4 were waited for; matrix products, arithmetic and copies ran while one was open for 1% of the time, Pallas kernels for 0%

commit v1 on v0

--- a/solution.py
+++ b/solution.py
@@ -119,31 +119,27 @@
     hidden_in = normal_one * params_main[3] + params_main[4]
     hidden_low = hidden_in.astype(jnp.bfloat16)
     dy = cotangent.astype(jnp.float32) * pad_mask.reshape(rows_all)[:, None].astype(jnp.float32)
-    zeta = product(lax.all_gather(hidden_low, "mp", axis=0, tiled=True), w_in) + params_hidden
+    in_all = lax.all_gather(w_in, "mp", axis=0, tiled=False)
+    back_all = lax.all_gather(w_back, "mp", axis=0, tiled=False)
+    bias_all = lax.all_gather(params_hidden, "mp", axis=0, tiled=False)
+    zeta = jnp.einsum("td,jdh->jth", hidden_low, in_all, preferred_element_type=jnp.float32) + bias_all[:, None, :]
     upper, gelu_pull = jax.vjp(gelu_exact, zeta)
     upper_low = upper.astype(jnp.bfloat16)
     ffn = (
-        lax.psum_scatter(
-            product(upper_low, w_back).astype(jnp.bfloat16), "mp", scatter_dimension=0, tiled=True
-        ).astype(jnp.float32)
+        jnp.einsum("jth,jhd->td", upper_low, back_all, preferred_element_type=jnp.float32)
         + params_main[5]
     )
     normal_two, factor_two = normed(hidden_in + ffn)
     dresid_two = norm_back(normal_two, factor_two, dy * params_main[6])
-    dupper = product(
-        lax.all_gather(dresid_two.astype(jnp.bfloat16), "mp", axis=0, tiled=True), w_back.T
+    dupper = jnp.einsum(
+        "td,jhd->jth", dresid_two.astype(jnp.bfloat16), back_all, preferred_element_type=jnp.float32
     )
     dzeta = gelu_pull(dupper)[0]
     dzeta_low = dzeta.astype(jnp.bfloat16)
-    dhidden = dresid_two + lax.psum_scatter(
-        product(dzeta_low, w_in.T).astype(jnp.bfloat16), "mp", scatter_dimension=0, tiled=True
-    ).astype(jnp.float32)
-    hidden_vec = lax.dynamic_update_slice_in_dim(
-        jnp.zeros((total_hidden,), jnp.float32),
-        jnp.sum(dzeta, axis=0),
-        lax.axis_index("mp") * width,
-        0,
-    )
+    dhidden = dresid_two + jnp.einsum(
+        "jth,jdh->td", dzeta_low, in_all, preferred_element_type=jnp.float32
+    )
+    hidden_vec = jnp.sum(dzeta, axis=1).reshape(total_hidden)
     activations = normal_two * params_main[6] + params_main[7]
     grad_gain_two = jnp.sum(dy * normal_two, axis=0)
     grad_shift_two = jnp.sum(dy, axis=0)

time: 1030 us -> 640 us (0.62)
  waiting for transfers between devices: 405 us -> 1.38 us
  matrix products: 364 us -> 379 us
  blocking collectives: 39.8 us -> 50.4 us
    reduce_scatter x2 -> x0, waiting for transfers between devices: 222 us -> none  [the longest x1 112 us: on_device(): lax.psum_scatter(product(upper_low, w_back).astype(jnp.bfloat16), 'mp', s...]
    all_gather x2, waiting for transfers between devices: 183 us -> 0.01 us  [the longest x1 0.01 us: on_device(): in_all = lax.all_gather(w_in, 'mp', axis=0, tiled=False)]
    dot_general x0 -> x4, matrix products: none -> 124 us  [the longest x1 47 us: on_device(): jnp.einsum('td,jdh->jth', hidden_low, in_all, preferred_element_type=jnp....]
    dot_general x12 -> x8, matrix products: 142 us -> 33.3 us  [product(): return jnp.dot(left, right, preferred_element_type=jnp.float32)]
    all_gather x0 -> x1, blocking collectives: none -> 10.4 us  [on_device(): bias_all = lax.all_gather(params_hidden, 'mp', axis=0, tiled=False)]
    unnamed x116 -> x120, local copies, waits for them, and re-layouts: 39.3 us -> 36.7 us
  transfers between devices with their start and end apart: 4 -> 2, of which waited for: 4 -> 0; matrix products, arithmetic and copies ran while one was open for 1% -> 30% of each run, Pallas kernels for 0% -> 0%
where the time goes in v1:
time: 640 us; the launch traced here: 638 us
  matrix products  379 us (59%)
  other arithmetic  117 us (18%)
  local copies, waits for them, and re-layouts  61.6 us (10%)
  blocking collectives  50.4 us (8%)
  between operations  17.3 us (3%)
  loops' own time  11.5 us (2%)
    dot_general x4, matrix products, scores_of(): jnp.einsum('qhd,khd->hqk', q_blk, k_seq, preferred_element_type=jnp.float32)  60.4 us
    convert_element_type x2, other arithmetic, one_step(): dscores = (probs * (dprobs - delta)).astype(jnp.bfloat16)  55.6 us
    dot_general x2, matrix products, one_step(): jnp.einsum('qhd,khd->hqk', d_blk, v_seq, preferred_element_type=jnp.float32)  51.9 us
    dot_general x1, matrix products, on_device(): jnp.einsum('td,jdh->jth', hidden_low, in_all, preferred_element_type=jnp....  47 us
    psum x1, blocking collectives, on_device(): grad_main, hidden_total = lax.psum((local_main, hidden_vec), ('dp', 'mp'))  40 us
    unnamed x120, local copies, waits for them, and re-layouts  36.7 us
    dot_general x1, matrix products, on_device(): jnp.einsum('td,jhd->jth', dresid_two.astype(jnp.bfloat16), back_all, pref...  36.6 us
    dot_general x2, matrix products, one_step(): jnp.einsum('hqk,qhd->khd', probs.astype(jnp.bfloat16), d_blk, preferred_e...  36.2 us
  transfers between devices with their start and end apart: 2, of which 0 were waited for; matrix products, arithmetic and copies ran while one was open for 30% of the time, Pallas kernels for 0%

profile of v1, /device:TPU:0, one launch (start us, length us, event | category | flops | bytes accessed | tf_op | source)
XLA Modules:
  0.0 637.5 jit_solution(2449860849833347566)
XLA Ops:
  14.8 5.9 add_convert_fusion.1
  20.7 6.4 reshape.302
  32.5 6.1 convolution_convert_fusion
  42.4 103.2 %while.50 = (s32[]{:T(128)}, bf16[2,512,16,64]{1,3,2,0:T(8,128)(2,1)}, f32[2,16,512]{2,1,0:T(8,128)S(1)}, s32[2]{0:T(128)S(1)}, s32[1024]{0:T(1024)S(1)}, /*inde...) while((s32[]{:T(128)}, ...), condition=%wide.region_3.4_spmd.clone.clone, body=%wide.region_0.3_spmd.clone.sunk.clone | while | flops 2250237440 | bytes 135549200 | solution.py:113
  46.5 15.8 %fusion.168 = (f32[16,512]{1,0:T(8,128)S(1)}, f32[16,512,1024]{2,1,0:T(8,128)}) fusion(pred[512,1024]{1,0:T(8,128)(4,1)S(1)} %fusion.167, bf16[1024,16,64]{0,2,1:T(8,128)(2,1)} %get-tuple-element.688, bf16[2,512,16,64]{1,3,2,0:T(8,128)(2,1)} %get-tuple-element.687, s32[]{:T(128)S(6)} %select_n.77), kind=kOutput, calls=%fused_computation.5.clone.1.clone | convolution fusion | flops 1098899456 | bytes 37257220 | tf_op jit(solution)/shard_map/while/body/eval_jaxpr/while/body/eval_jaxpr/qhd,khd->hqk/dot_general | solution.py:97
  62.3 15.9 %fusion.169 = f32[16,512]{1,0:T(8,128)S(1)} fusion(f32[16,512,1024]{2,1,0:T(8,128)} %get-tuple-element.615, f32[16,512]{1,0:T(8,128)S(1)} %get-tuple-element.616, pred[512,1024]{1,0:T(8,128)(4,1)S(1)} %fusion.167), kind=kLoop, calls=%fused_computation.6.clone.1.clone | loop fusion | flops 33546240 | bytes 34144256 | tf_op jit(solution)/shard_map/while/body/eval_jaxpr/while/body/eval_jaxpr/reduce_sum | solution.py:108
  78.2 14.6 %bitcast_dynamic-update-slice_fusion.9 = bf16[2,512,16,64]{1,3,2,0:T(8,128)(2,1)S(1)} fusion(bf16[2,512,16,64]{1,3,2,0:T(8,128)(2,1)S(1)} %copy-done.10, s32[]{:T(128)S(6)} %copy.110, bf16[1024,16,64]{0,2,1:T(8,128)(2,1)S(1)} %copy-done.3, f32[16,512,1024]{2,1,0:T(8,128)} %get-tuple-element.615, f32[16,512]{1,0:T(8,128)S(1)} %fusion.169, ...), kind=kOutput, calls=%fused_computation.8.clone.1.clone | convolution fusion | flops 1115684864 | bytes 38338564 | tf_op jit(solution)/shard_map/while/body/eval_jaxpr/while/body/eval_jaxpr/hqk,khd->qhd/dot_general | solution.py:110
  98.2 15.8 %fusion.168 = (f32[16,512]{1,0:T(8,128)S(1)}, f32[16,512,1024]{2,1,0:T(8,128)}) fusion(pred[512,1024]{1,0:T(8,128)(4,1)S(1)} %fusion.167, bf16[1024,16,64]{0,2,1:T(8,128)(2,1)} %get-tuple-element.688, bf16[2,512,16,64]{1,3,2,0:T(8,128)(2,1)} %get-tuple-element.687, s32[]{:T(128)S(6)} %select_n.77), kind=kOutput, calls=%fused_computation.5.clone.1.clone | convolution fusion | flops 1098899456 | bytes 37257220 | tf_op jit(solution)/shard_map/while/body/eval_jaxpr/while/body/eval_jaxpr/qhd,khd->hqk/dot_general | solution.py:97
  114.0 15.5 %fusion.169 = f32[16,512]{1,0:T(8,128)S(1)} fusion(f32[16,512,1024]{2,1,0:T(8,128)} %get-tuple-element.615, f32[16,512]{1,0:T(8,128)S(1)} %get-tuple-element.616, pred[512,1024]{1,0:T(8,128)(4,1)S(1)} %fusion.167), kind=kLoop, calls=%fused_computation.6.clone.1.clone | loop fusion | flops 33546240 | bytes 34144256 | tf_op jit(solution)/shard_map/while/body/eval_jaxpr/while/body/eval_jaxpr/reduce_sum | solution.py:108
  129.5 14.6 %bitcast_dynamic-update-slice_fusion.9 = bf16[2,512,16,64]{1,3,2,0:T(8,128)(2,1)S(1)} fusion(bf16[2,512,16,64]{1,3,2,0:T(8,128)(2,1)S(1)} %copy-done.10, s32[]{:T(128)S(6)} %copy.110, bf16[1024,16,64]{0,2,1:T(8,128)(2,1)S(1)} %copy-done.3, f32[16,512,1024]{2,1,0:T(8,128)} %get-tuple-element.615, f32[16,512]{1,0:T(8,128)S(1)} %fusion.169, ...), kind=kOutput, calls=%fused_computation.8.clone.1.clone | convolution fusion | flops 1115684864 | bytes 38338564 | tf_op jit(solution)/shard_map/while/body/eval_jaxpr/while/body/eval_jaxpr/hqk,khd->qhd/dot_general | solution.py:110
  159.4 10.4 %all-gather.3 = f32[8,1,512]{2,1,0:T(1,128)S(1)} all-gather(f32[1,1,512]{2,1,0:T(1,128)S(1)} %bitcast.296), channel_id=3, replica_groups=mesh['dp'=4,'mp'=8] {'mp'}, dimensions={0}, use_global_device_ids=true | all-gather | bytes 18432 | tf_op jit(solution)/shard_map/all_gather | solution.py:124
  175.3 47.0 %fusion.39 = (f32[8,1024,512]{2,1,0:T(8,128)}, f32[1024,8,512]{2,0,1:T(8,128)}) fusion(f32[8,512]{1,0:T(8,128)S(1)} %bitcast.293, bf16[8,1024,512]{2,1,0:T(8,128)(2,1)} %bitcast.303, bf16[1024,1024,1]{0,1,2:T(8,128)(2,1)} %fusion.77.clone.4), kind=kOutput, calls=%fused_computation.53 | convolution fusion | flops 8854175744 | bytes 44056576 | tf_op jit(solution)/shard_map/td,jdh->jth/dot_general | solution.py:125
  222.4 22.1 %fusion.100 = (f32[1024]{0:T(1024)S(1)}, f32[1024,1024]{0,1:T(8,128)}) fusion(f32[1024]{0:T(1024)S(1)} %bitcast.299, bf16[8,512,1024]{2,1,0:T(8,128)(2,1)} %bitcast.305, f32[8,1024,512]{2,1,0:T(8,128)} %get-tuple-element.458, f32[1024,8,512]{2,0,1:T(8,128)} %get-tuple-element.459, f32[8,512]{1,0:T(8,128)S(1)} %bitcast.294, f32[1024]{0:T(1024)S(1)} %bitcast.291, ...), kind=kOutput, calls=%fused_computation.154 | convolution fusion | flops 8614050816 | bytes 50372608 | tf_op jit(solution)/shard_map/jth,jhd->td/dot_general | solution.py:129
  249.1 36.6 %fusion.101 = (f32[8,512]{1,0:T(8,128)}, bf16[8,1024,512]{2,1,0:T(8,128)(2,1)}) fusion(f32[8,1024,512]{2,1,0:T(8,128)} %get-tuple-element.458, bf16[8,512,1024]{2,1,0:T(8,128)(2,1)} %bitcast.306, f32[1024]{0:T(1024)S(1)} %get-tuple-element.465, f32[1024,1024]{0,1:T(8,128)} %get-tuple-element.461, f32[1024]{0:T(1024)S(1)} %broadcast_multiply_fusion.5, ...), kind=kOutput, calls=%fused_computation.155 | convolution fusion | flops 8667525120 | bytes 56680448 | tf_op jit(solution)/shard_map/td,jhd->jth/dot_general | solution.py:134
  285.7 6.6 %multiply_reduce_fusion.1 = (f32[1024]{0:T(1024)}, f32[1024]{0:T(1024)}, f32[1024]{0:T(1024)}, f32[1024,1024]{0,1:T(8,128)}) fusion(bf16[1024,1024]{0,1:T(8,128)(2,1)} %copy.71, f32[1024,1024]{0,1:T(8,128)} %get-tuple-element.461, f32[1024]{0:T(1024)S(1)} %copy-done.32, f32[1024]{0:T(1024)S(1)} %add_rsqrt_fusion, f32[1024]{0:T(1024)S(1)} %broadcast_multiply_fusion.5, ...), kind=kLoop, calls=%fused_computation.90 | loop fusion | flops 15725568 | bytes 10526720 | tf_op jit(solution)/shard_map/reduce_sum | solution.py:144
  297.7 18.2 %multiply_reduce_fusion.2 = (f32[1024]{0:T(1024)}, f32[1024]{0:T(1024)S(1)}, f32[1024]{0:T(1024)S(1)}, f32[1024]{0:T(1024)}, f32[1024,1024]{0,1:T(8,128)S(1)}) fusion(f32[1024,1024]{0,1:T(8,128)} %get-tuple-element.457, f32[1024]{0:T(1024)S(1)} %copy-done.34, f32[1024]{0:T(1024)S(1)} %copy-done.28, f32[1024]{0:T(1024)S(1)} %bitcast.279, ...), kind=kOutput, calls=%fused_computation.91 | convolution fusion | flops 8609853440 | bytes 31510528 | tf_op jit(solution)/shard_map/jth,jdh->td/dot_general | solution.py:139
  323.6 6.3 reshape.301
  329.9 5.6 copy.76
  335.5 224.7 %while.51 = (s32[]{:T(128)}, f32[1024,16,64]{0,2,1:T(8,128)}, f32[1024,16,64]{0,2,1:T(8,128)}, f32[2,512,16,64]{1,3,2,0:T(8,128)}, s32[2]{0:T(128)S(1)}, /*index...) while((s32[]{:T(128)}, f32[1024,16,64]{0,2,1:T(8,128)}, ...), condition=%wide.region_14.15_spmd.clone.clone, body=%wide.region_12.14_spmd.clone.sunk.clone | while | flops 5502395904 | bytes 283365632 | solution.py:181
  338.5 14.4 %fusion.179 = f32[16,512,1024]{2,1,0:T(8,128)} fusion(bf16[1024,16,64]{0,2,1:T(8,128)(2,1)S(1)} %get-tuple-element.722, bf16[2,512,16,64]{1,3,2,0:T(8,128)(2,1)} %get-tuple-element.719, s32[]{:T(128)S(6)} %select_n.81), kind=kOutput, calls=%fused_computation.37.clone.1.clone | convolution fusion | flops 1073741824 | bytes 36700164 | tf_op jit(solution)/shard_map/while/body/eval_jaxpr/while/body/eval_jaxpr/qhd,khd->hqk/dot_general | solution.py:97
  354.3 25.9 %multiply_reduce_fusion.12 = (f32[16,512]{1,0:T(8,128)S(1)}, f32[16,512,1024]{2,1,0:T(8,128)}) fusion(f32[16,512,1024]{2,1,0:T(8,128)} %fusion.179, f32[16,512]{1,0:T(8,128)S(1)} %dynamic-slice_bitcast_fusion.3, pred[512,1024]{1,0:T(8,128)(4,1)S(1)} %fusion.180, bf16[1024,16,64]{0,2,1:T(8,128)(2,1)} %get-tuple-element.725, ...), kind=kOutput, calls=%fused_computation.22.clone.1.clone | convolution fusion | flops 1115676672 | bytes 70844416 | tf_op jit(solution)/shard_map/while/body/eval_jaxpr/while/body/eval_jaxpr/qhd,khd->hqk/dot_general | solution.py:163
  380.3 27.8 %multiply_convert_fusion.3 = bf16[16,512,1024]{2,1,0:T(8,128)(2,1)} fusion(f32[16,512,1024]{2,1,0:T(8,128)} %get-tuple-element.644, f32[16,512,1024]{2,1,0:T(8,128)} %fusion.179, f32[16,512]{1,0:T(8,128)S(1)} %get-tuple-element.645, f32[16,512]{1,0:T(8,128)S(1)} %dynamic-slice_bitcast_fusion.3, pred[512,1024]{1,0:T(8,128)(4,1)S(1)} %fusion.180), kind=kLoop, calls=%fused_computation.21.clone.1.clone | loop fusion | flops 50331648 | bytes 84475904 | tf_op jit(solution)/shard_map/while/body/eval_jaxpr/while/body/eval_jaxpr/convert_element_type | solution.py:165
  408.1 11.1 %bitcast_add_fusion.8 = f32[1024,16,64]{0,2,1:T(8,128)} fusion(f32[1024,16,64]{0,2,1:T(8,128)} %get-tuple-element.703, bf16[16,512,1024]{2,1,0:T(8,128)(2,1)} %multiply_convert_fusion.3, pred[]{:T(512)S(6)} %compare.4, bf16[2,512,16,64]{1,3,2,0:T(8,128)(2,1)} %get-tuple-element.719, s32[]{:T(128)S(6)} %select_n.81), kind=kOutput, calls=%fused_computation.28.clone.1.clone | convolution fusion | flops 1076887552 | bytes 26214404 | tf_op jit(solution)/shard_map/while/body/eval_jaxpr/while/body/eval_jaxpr/hqk,qhd->khd/dot_general | solution.py:169
  419.2 17.5 %bitcast_add_fusion.9 = f32[1024,16,64]{0,2,1:T(8,128)} fusion(f32[1024,16,64]{0,2,1:T(8,128)} %get-tuple-element.704, f32[16,512,1024]{2,1,0:T(8,128)} %fusion.179, f32[16,512]{1,0:T(8,128)S(1)} %dynamic-slice_bitcast_fusion.3, pred[512,1024]{1,0:T(8,128)(4,1)S(1)} %fusion.180, pred[]{:T(512)S(6)} %compare.4, ...), kind=kOutput, calls=%fused_computation.27.clone.1.clone | convolution fusion | flops 1109393408 | bytes 43548676 | tf_op jit(solution)/shard_map/while/body/eval_jaxpr/while/body/eval_jaxpr/hqk,qhd->khd/dot_general | solution.py:172
  436.7 10.2 %bitcast_dynamic-update-slice_fusion.11 = f32[2,512,16,64]{1,3,2,0:T(8,128)} fusion(f32[2,512,16,64]{1,3,2,0:T(8,128)} %get-tuple-element.705, s32[]{:T(128)S(6)} %copy.120, bf16[16,512,1024]{2,1,0:T(8,128)(2,1)} %multiply_convert_fusion.3, bf16[1024,16,64]{0,2,1:T(8,128)(2,1)S(1)} %get-tuple-element.722), kind=kOutput, calls=%fused_computation.29.clone.1.clone | convolution fusion | flops 1074266112 | bytes 20971524 | tf_op jit(solution)/shard_map/while/body/eval_jaxpr/while/body/eval_jaxpr/hqk,khd->qhd/dot_general | solution.py:166
  449.4 14.4 %fusion.179 = f32[16,512,1024]{2,1,0:T(8,128)} fusion(bf16[1024,16,64]{0,2,1:T(8,128)(2,1)S(1)} %get-tuple-element.722, bf16[2,512,16,64]{1,3,2,0:T(8,128)(2,1)} %get-tuple-element.719, s32[]{:T(128)S(6)} %select_n.81), kind=kOutput, calls=%fused_computation.37.clone.1.clone | convolution fusion | flops 1073741824 | bytes 36700164 | tf_op jit(solution)/shard_map/while/body/eval_jaxpr/while/body/eval_jaxpr/qhd,khd->hqk/dot_general | solution.py:97
  465.2 25.9 %multiply_reduce_fusion.12 = (f32[16,512]{1,0:T(8,128)S(1)}, f32[16,512,1024]{2,1,0:T(8,128)}) fusion(f32[16,512,1024]{2,1,0:T(8,128)} %fusion.179, f32[16,512]{1,0:T(8,128)S(1)} %dynamic-slice_bitcast_fusion.3, pred[512,1024]{1,0:T(8,128)(4,1)S(1)} %fusion.180, bf16[1024,16,64]{0,2,1:T(8,128)(2,1)} %get-tuple-element.725, ...), kind=kOutput, calls=%fused_computation.22.clone.1.clone | convolution fusion | flops 1115676672 | bytes 70844416 | tf_op jit(solution)/shard_map/while/body/eval_jaxpr/while/body/eval_jaxpr/qhd,khd->hqk/dot_general | solution.py:163
  491.2 27.8 %multiply_convert_fusion.3 = bf16[16,512,1024]{2,1,0:T(8,128)(2,1)} fusion(f32[16,512,1024]{2,1,0:T(8,128)} %get-tuple-element.644, f32[16,512,1024]{2,1,0:T(8,128)} %fusion.179, f32[16,512]{1,0:T(8,128)S(1)} %get-tuple-element.645, f32[16,512]{1,0:T(8,128)S(1)} %dynamic-slice_bitcast_fusion.3, pred[512,1024]{1,0:T(8,128)(4,1)S(1)} %fusion.180), kind=kLoop, calls=%fused_computation.21.clone.1.clone | loop fusion | flops 50331648 | bytes 84475904 | tf_op jit(solution)/shard_map/while/body/eval_jaxpr/while/body/eval_jaxpr/convert_element_type | solution.py:165
  518.9 12.3 %bitcast_add_fusion.8 = f32[1024,16,64]{0,2,1:T(8,128)} fusion(f32[1024,16,64]{0,2,1:T(8,128)} %get-tuple-element.703, bf16[16,512,1024]{2,1,0:T(8,128)(2,1)} %multiply_convert_fusion.3, pred[]{:T(512)S(6)} %compare.4, bf16[2,512,16,64]{1,3,2,0:T(8,128)(2,1)} %get-tuple-element.719, s32[]{:T(128)S(6)} %select_n.81), kind=kOutput, calls=%fused_computation.28.clone.1.clone | convolution fusion | flops 1076887552 | bytes 26214404 | tf_op jit(solution)/shard_map/while/body/eval_jaxpr/while/body/eval_jaxpr/hqk,qhd->khd/dot_general | solution.py:169
  531.3 18.7 %bitcast_add_fusion.9 = f32[1024,16,64]{0,2,1:T(8,128)} fusion(f32[1024,16,64]{0,2,1:T(8,128)} %get-tuple-element.704, f32[16,512,1024]{2,1,0:T(8,128)} %fusion.179, f32[16,512]{1,0:T(8,128)S(1)} %dynamic-slice_bitcast_fusion.3, pred[512,1024]{1,0:T(8,128)(4,1)S(1)} %fusion.180, pred[]{:T(512)S(6)} %compare.4, ...), kind=kOutput, calls=%fused_computation.27.clone.1.clone | convolution fusion | flops 1109393408 | bytes 43548676 | tf_op jit(solution)/shard_map/while/body/eval_jaxpr/while/body/eval_jaxpr/hqk,qhd->khd/dot_general | solution.py:172
  550.0 10.1 %bitcast_dynamic-update-slice_fusion.11 = f32[2,512,16,64]{1,3,2,0:T(8,128)} fusion(f32[2,512,16,64]{1,3,2,0:T(8,128)} %get-tuple-element.705, s32[]{:T(128)S(6)} %copy.120, bf16[16,512,1024]{2,1,0:T(8,128)(2,1)} %multiply_convert_fusion.3, bf16[1024,16,64]{0,2,1:T(8,128)(2,1)S(1)} %get-tuple-element.722), kind=kOutput, calls=%fused_computation.29.clone.1.clone | convolution fusion | flops 1074266112 | bytes 20971524 | tf_op jit(solution)/shard_map/while/body/eval_jaxpr/while/body/eval_jaxpr/hqk,khd->qhd/dot_general | solution.py:166
  584.2 40.0 %all-reduce = (f32[8,1024]{1,0:T(8,128)S(1)}, f32[4096]{0:T(1024)S(1)}) all-reduce(f32[8,1024]{1,0:T(8,128)S(1)} %stack.35, f32[4096]{0:T(1024)S(1)} %bitcast.276), channel_id=1, replica_groups=mesh['dp'=4,'mp'=8] {'dp','mp'}, use_global_device_ids=true, to_apply=%region_23.24 | all-reduce | flops 12288 | bytes 98304 | tf_op jit(solution)/shard_map/psum | solution.py:205
  (202 shorter events, 89.1 us)
Async XLA Ops:
  7.2 143.0 %copy-start = (bf16[1024,1024]{1,0:T(8,128)(2,1)S(1)}, bf16[1024,1024]{1,0:T(8,128)(2,1)}, u32[]{:S(2)}) copy-start(bf16[1024,1024]{1,0:T(8,128)(2,1)} %param.29) | copy-start | bytes 6291460
  7.2 168.1 %all-gather.7.cloned.1.call-start = ((), (), s32[]{:S(2)}) async-start(), calls=%async_computation | async-start | bytes 9437184 | tf_op jit(solution)/shard_map/all_gather | solution.py:122
  7.9 214.4 %all-gather.9.cloned.1.call-start = ((), (), s32[]{:S(2)}) async-start(), calls=%async_computation.1 | async-start | bytes 9437184 | tf_op jit(solution)/shard_map/all_gather | solution.py:123
  32.5 6.1 copy-start.12
  32.5 6.1 copy-start.16
  62.3 15.9 %copy-start.3 = (bf16[1024,16,64]{0,2,1:T(8,128)(2,1)S(1)}, bf16[1024,16,64]{0,2,1:T(8,128)(2,1)}, u32[]{:S(2)}) copy-start(bf16[1024,16,64]{0,2,1:T(8,128)(2,1)} %get-tuple-element.689) | copy-start | bytes 6291460 | tf_op jit(solution)/shard_map/while/body/eval_jaxpr/while
  62.3 15.9 %copy-start.10 = (bf16[2,512,16,64]{1,3,2,0:T(8,128)(2,1)S(1)}, bf16[2,512,16,64]{1,3,2,0:T(8,128)(2,1)}, u32[]{:S(2)}) copy-start(bf16[2,512,16,64]{1,3,2,0:T(8,128)(2,1)} %get-tuple-element.673) | copy-start | bytes 6291460 | tf_op jit(solution)/shard_map/while/body/eval_jaxpr/while
  114.0 15.5 %copy-start.3 = (bf16[1024,16,64]{0,2,1:T(8,128)(2,1)S(1)}, bf16[1024,16,64]{0,2,1:T(8,128)(2,1)}, u32[]{:S(2)}) copy-start(bf16[1024,16,64]{0,2,1:T(8,128)(2,1)} %get-tuple-element.689) | copy-start | bytes 6291460 | tf_op jit(solution)/shard_map/while/body/eval_jaxpr/while
  114.0 15.5 %copy-start.10 = (bf16[2,512,16,64]{1,3,2,0:T(8,128)(2,1)S(1)}, bf16[2,512,16,64]{1,3,2,0:T(8,128)(2,1)}, u32[]{:S(2)}) copy-start(bf16[2,512,16,64]{1,3,2,0:T(8,128)(2,1)} %get-tuple-element.673) | copy-start | bytes 6291460 | tf_op jit(solution)/shard_map/while/body/eval_jaxpr/while
  155.5 17.8 %copy-start.29 = (f32[1,1024]{1,0:T(1,128)S(1)}, f32[1,1024]{1,0:T(1,128)}, u32[]{:S(2)}) copy-start(f32[1,1024]{1,0:T(1,128)} %get-tuple-element.451) | copy-start | bytes 12292
  155.5 17.8 %copy-start.43 = (f32[1,1024]{1,0:T(1,128)S(1)}, f32[1,1024]{1,0:T(1,128)}, u32[]{:S(2)}) copy-start(f32[1,1024]{1,0:T(1,128)} %get-tuple-element.450) | copy-start | bytes 12292
  175.3 47.1 %copy-start.28 = (f32[1024]{0:T(1024)S(1)}, f32[1024]{0:T(1024)}, u32[]{:S(2)}) copy-start(f32[1024]{0:T(1024)} %copy-done.27) | copy-start | bytes 12292
  175.3 47.1 %copy-start.30 = (f32[1,1024]{1,0:T(1,128)S(1)}, f32[1,1024]{1,0:T(1,128)}, u32[]{:S(2)}) copy-start(f32[1,1024]{1,0:T(1,128)} %get-tuple-element.451) | copy-start | bytes 12292
  175.3 47.1 %copy-start.34 = (f32[1024]{0:T(1024)S(1)}, f32[1024]{0:T(1024)}, u32[]{:S(2)}) copy-start(f32[1024]{0:T(1024)} %copy-done.33) | copy-start | bytes 12292
  175.3 47.1 %copy-start.44 = (f32[1,1024]{1,0:T(1,128)S(1)}, f32[1,1024]{1,0:T(1,128)}, u32[]{:S(2)}) copy-start(f32[1,1024]{1,0:T(1,128)} %get-tuple-element.450) | copy-start | bytes 12292
  175.3 47.1 %copy-start.51 = (f32[1,1024]{1,0:T(1,128)S(1)}, f32[1,1024]{1,0:T(1,128)}, u32[]{:S(2)}) copy-start(f32[1,1024]{1,0:T(1,128)} %get-tuple-element.449) | copy-start | bytes 12292
  222.4 25.0 %copy-start.9 = (bf16[1024,1024]{0,1:T(8,128)(2,1)S(1)}, bf16[1024,1024]{0,1:T(8,128)(2,1)}, u32[]{:S(2)}) copy-start(bf16[1024,1024]{0,1:T(8,128)(2,1)} %copy.71) | copy-start | bytes 6291460
  249.1 36.6 %copy-start.38 = (f32[1,1024]{1,0:T(1,128)S(1)}, f32[1,1024]{1,0:T(1,128)}, u32[]{:S(2)}) copy-start(f32[1,1024]{1,0:T(1,128)} %get-tuple-element.455) | copy-start | bytes 12292
  297.7 18.2 %copy-start.5 = (f32[1024,1024]{0,1:T(8,128)S(1)}, f32[1024,1024]{0,1:T(8,128)}, u32[]{:S(2)}) copy-start(f32[1024,1024]{0,1:T(8,128)} %get-tuple-element.457) | copy-start | bytes 12582916
  574.0 55.4 %copy-start.1 = (bf16[1024,1024]{1,0:T(8,128)(2,1)S(1)}, bf16[1024,1024]{1,0:T(8,128)(2,1)}, u32[]{:S(2)}) copy-start(bf16[1024,1024]{1,0:T(8,128)(2,1)} %param.29) | copy-start | bytes 6291460
  578.4 5.7 copy-start.41
  578.4 5.7 copy-start.42
  578.4 5.7 copy-start.49
  578.4 5.7 copy-start.50
  578.4 48.4 %copy-start.25 = (f32[8,1024]{1,0:T(8,128)S(1)}, f32[8,1024]{1,0:T(8,128)}, u32[]{:S(2)}) copy-start(f32[8,1024]{1,0:T(8,128)} %param.32) | copy-start | bytes 98308
  578.4 48.4 %copy-start.35 = (f32[8,1024]{1,0:T(8,128)S(1)}, f32[8,1024]{1,0:T(8,128)}, u32[]{:S(2)}) copy-start(f32[8,1024]{1,0:T(8,128)} %param.38) | copy-start | bytes 98308
  578.4 48.4 %copy-start.36 = (f32[8,1024]{1,0:T(8,128)S(1)}, f32[8,1024]{1,0:T(8,128)}, u32[]{:S(2)}) copy-start(f32[8,1024]{1,0:T(8,128)} %param.35) | copy-start | bytes 98308
  578.4 48.4 %copy-start.37 = (f32[8,1024]{1,0:T(8,128)S(1)}, f32[8,1024]{1,0:T(8,128)}, u32[]{:S(2)}) copy-start(f32[8,1024]{1,0:T(8,128)} %param.34) | copy-start | bytes 98308
  578.5 49.6 %copy-start.47 = (f32[512]{0:T(512)S(1)}, f32[512]{0:T(512)}, u32[]{:S(2)}) copy-start(f32[512]{0:T(512)} %param.33) | copy-start | bytes 6148
  578.5 49.6 %copy-start.53 = (f32[512]{0:T(512)S(1)}, f32[512]{0:T(512)}, u32[]{:S(2)}) copy-start(f32[512]{0:T(512)} %param.39) | copy-start | bytes 6148
  578.5 49.6 %copy-start.54 = (f32[512]{0:T(512)S(1)}, f32[512]{0:T(512)}, u32[]{:S(2)}) copy-start(f32[512]{0:T(512)} %param.37) | copy-start | bytes 6148
  578.5 49.6 %copy-start.55 = (f32[512]{0:T(512)S(1)}, f32[512]{0:T(512)}, u32[]{:S(2)}) copy-start(f32[512]{0:T(512)} %param.36) | copy-start | bytes 6148
  (31 other events, 108.1 us)
Sparse Core Ops, SparseCore 0:
  9.9 57.0 all-gather.6
  68.9 54.3 all-gather.8

commit v2 on v1

v2 whole, which is shorter than its diff:
```python
import functools
import math

import jax
import jax.numpy as jnp
from jax import lax
from jax.experimental import pallas as pl
from jax.experimental.pallas import tpu as pltpu
from jax.sharding import PartitionSpec as P

STEP = 5
f32, bf16 = jnp.float32, jnp.bfloat16
NN = (((1,), (0,)), ((), ()))
NT = (((1,), (1,)), ((), ()))
DN_NT = NT

BLK = 128
PAIR = 128
NEG = -1e9
ALLOWED = (2, 3, 4, 5, 6, 8)


def windows(seg_row, blk, allowed):
    length = seg_row.shape[0]
    nb = length // blk
    first = seg_row[::blk]
    last = seg_row[blk - 1 :: blk]
    lo = jnp.sum(seg_row[None, :] < first[:, None], axis=1)
    hi = jnp.sum(seg_row[None, :] <= last[:, None], axis=1)
    start = lo // blk
    count = (hi + blk - 1) // blk - start
    allowed_arr = jnp.array(allowed)
    variant = jnp.sum(allowed_arr[None, :] < count[:, None], axis=1)
    size = allowed_arr[variant]
    start = jnp.minimum(start, nb - size)
    return jnp.stack([start, variant]).astype(jnp.int32)


def halves(x):
    lane = lax.broadcasted_iota(jnp.int32, x.shape, 1)
    zero = jnp.zeros_like(x)
    return jnp.concatenate([jnp.where(lane < 64, x, zero), jnp.where(lane >= 64, x, zero)], axis=0)


def fill_bias(bias_ref, segcol_ref, segrow_ref, i, start, width):
    rows = pl.ds(start * BLK, width)
    kcode = segcol_ref[rows, :]
    qseg = segrow_ref[:, pl.ds(pl.multiple_of(i * BLK, BLK), BLK)]
    kpos = start * BLK + lax.broadcasted_iota(jnp.int32, (width, BLK), 0)
    qpos = i * BLK + lax.broadcasted_iota(jnp.int32, (width, BLK), 1)
    vis = (kcode == qseg) | (kpos == qpos)
    bias_ref[pl.ds(0, width), :] = jnp.where(vis, 0.0, NEG).astype(f32)


def fwd_kernel(allowed, npair, unroll, win_ref, q_ref, k_ref, v_ref, segcol_ref, segrow_ref, o_ref, lse_ref, vt_ref, bias_ref):
    i = pl.program_id(0)

    @pl.when(i == 0)
    def _():
        for h in range(npair):
            vt_ref[h * PAIR : (h + 1) * PAIR, :] = v_ref[:, h * PAIR : (h + 1) * PAIR].T

    start = win_ref[0, i]
    variant = win_ref[1, i]
    for n, size in enumerate(allowed):
        width = size * BLK

        @pl.when(variant == n)
        def _(width=width):
            fill_bias(bias_ref, segcol_ref, segrow_ref, i, start, width)
            rows = pl.ds(pl.multiple_of(start * BLK, BLK), width)

            def pair(h):
                cols = pl.ds(pl.multiple_of(h * PAIR, PAIR), PAIR)
                qbd = halves(q_ref[:, cols])
                s = lax.dot_general(k_ref[rows, cols], qbd, DN_NT, preferred_element_type=f32)
                b = bias_ref[pl.ds(0, width), :]
                s = s * 0.125 + jnp.concatenate([b, b], axis=1)
                top = jnp.max(s, axis=0, keepdims=True)
                p = jnp.exp(s - top)
                tot = jnp.sum(p, axis=0, keepdims=True)
                ot = lax.dot_general(
                    vt_ref[cols, rows], p.astype(bf16), (((1,), (0,)), ((), ())), preferred_element_type=f32
                )
                ot = ot * (1.0 / tot)
                ot = jnp.concatenate([ot[:64, :BLK], ot[64:, BLK:]], axis=0)
                o_ref[:, cols] = ot.T.astype(bf16)
                lse_ref[0, pl.ds(h, 1), :] = top + jnp.log(tot)

            def body(t, c):
                for u in range(unroll):
                    pair(t * unroll + u)
                return c

            lax.fori_loop(0, npair // unroll, body, 0)


def attn_fwd(q, k, v, seg, pad, allowed=(1, 2, 3, 4, 5, 6, 7, 8), unroll=1):
    length, d = q.shape
    nb, npair = length // BLK, d // PAIR
    win = windows(seg, BLK, allowed)
    segcol = jnp.where(pad == 1, seg, -1)[:, None]
    full = lambda: pl.BlockSpec((length, d), lambda i, w: (0, 0))
    return pl.pallas_call(
        functools.partial(fwd_kernel, allowed, npair, unroll),
        out_shape=(jax.ShapeDtypeStruct((length, d), bf16), jax.ShapeDtypeStruct((nb, npair, 2 * BLK), f32)),
        grid_spec=pltpu.PrefetchScalarGridSpec(
            num_scalar_prefetch=1, grid=(nb,),
            in_specs=[pl.BlockSpec((BLK, d), lambda i, w: (i, 0)), full(), full(),
                      pl.BlockSpec((length, 1), lambda i, w: (0, 0)), pl.BlockSpec((1, length), lambda i, w: (0, 0))],
            out_specs=[pl.BlockSpec((BLK, d), lambda i, w: (i, 0)), pl.BlockSpec((1, npair, 2 * BLK), lambda i, w: (i, 0, 0))],
            scratch_shapes=[pltpu.VMEM((d, length), bf16), pltpu.VMEM((length, BLK), f32)]),
        compiler_params=pltpu.CompilerParams(vmem_limit_bytes=48 << 20),
        name="attend",
    )(win, q, k, v, segcol, seg[None, :])


def bwd_kernel(allowed, npair, unroll, win_ref, q_ref, k_ref, v_ref, do_ref, lse_ref, segcol_ref, segrow_ref,
               dq_ref, dk_ref, dv_ref, kt_ref, bias_ref):
    i = pl.program_id(0)

    @pl.when(i == 0)
    def _():
        for h in range(npair):
            kt_ref[h * PAIR : (h + 1) * PAIR, :] = k_ref[:, h * PAIR : (h + 1) * PAIR].T
        dk_ref[...] = jnp.zeros_like(dk_ref)
        dv_ref[...] = jnp.zeros_like(dv_ref)

    start = win_ref[0, i]
    variant = win_ref[1, i]
    for n, size in enumerate(allowed):
        width = size * BLK

        @pl.when(variant == n)
        def _(width=width):
            fill_bias(bias_ref, segcol_ref, segrow_ref, i, start, width)
            rows = pl.ds(pl.multiple_of(start * BLK, BLK), width)

            def pair(h):
                cols = pl.ds(pl.multiple_of(h * PAIR, PAIR), PAIR)
                qbd = halves(q_ref[:, cols])
                dobd = halves(do_ref[:, cols])
                s = lax.dot_general(k_ref[rows, cols], qbd, DN_NT, preferred_element_type=f32)
                dp = lax.dot_general(v_ref[rows, cols], dobd, DN_NT, preferred_element_type=f32)
                b = bias_ref[pl.ds(0, width), :]
                lse = lse_ref[0, pl.ds(h, 1), :]
                p = jnp.exp(s * 0.125 + jnp.concatenate([b, b], axis=1) - lse)
                t = p * dp
                delta = jnp.sum(t, axis=0, keepdims=True)
                ds = (t - p * delta).astype(bf16)
                nn = (((1,), (0,)), ((), ()))
                dv_ref[rows, cols] += lax.dot_general(p.astype(bf16), dobd, nn, preferred_element_type=f32)
                dk_ref[rows, cols] += 0.125 * lax.dot_general(ds, qbd, nn, preferred_element_type=f32)
                dqt = lax.dot_general(kt_ref[cols, rows], ds, nn, preferred_element_type=f32)
                dqt = jnp.concatenate([dqt[:64, :BLK], dqt[64:, BLK:]], axis=0)
                dq_ref[:, cols] = 0.125 * dqt.T

            def body(t, c):
                for u in range(unroll):
                    pair(t * unroll + u)
                return c

            lax.fori_loop(0, npair // unroll, body, 0)


def attn_bwd(q, k, v, do, lse, seg, pad, allowed=(1, 2, 3, 4, 5, 6, 7, 8), unroll=1):
    length, d = q.shape
    nb, npair = length // BLK, d // PAIR
    win = windows(seg, BLK, allowed)
    segcol = jnp.where(pad == 1, seg, -1)[:, None]
    full = lambda: pl.BlockSpec((length, d), lambda i, w: (0, 0))
    row = lambda: pl.BlockSpec((BLK, d), lambda i, w: (i, 0))
    return pl.pallas_call(
        functools.partial(bwd_kernel, allowed, npair, unroll),
        out_shape=tuple(jax.ShapeDtypeStruct((length, d), f32) for _ in range(3)),
        grid_spec=pltpu.PrefetchScalarGridSpec(
            num_scalar_prefetch=1, grid=(nb,),
            in_specs=[row(), full(), full(), row(), pl.BlockSpec((1, npair, 2 * BLK), lambda i, w: (i, 0, 0)),
                      pl.BlockSpec((length, 1), lambda i, w: (0, 0)), pl.BlockSpec((1, length), lambda i, w: (0, 0))],
            out_specs=[row(), full(), full()],
            scratch_shapes=[pltpu.VMEM((d, length), bf16), pltpu.VMEM((length, BLK), f32)]),
        compiler_params=pltpu.CompilerParams(vmem_limit_bytes=56 << 20),
        name="attend_back",
    )(win, q, k, v, do, lse, segcol, seg[None, :])


def dot(a, b, dims=NN):
    return lax.dot_general(a, b, dims, preferred_element_type=f32)


def gelu_both(z):
    x = jnp.abs(z) * 0.7071067811865476
    e = jnp.exp(-0.5 * z * z)
    t = 1.0 / (1.0 + 0.3275911 * x)
    poly = t * (0.254829592 + t * (-0.284496736 + t * (1.421413741 + t * (-1.453152027 + t * 1.061405429))))
    tail = 0.5 * poly * e
    phi = jnp.where(z >= 0, 1.0 - tail, tail)
    return z * phi, phi + z * (0.3989422804014327 * e)


def normed(r):
    center = r - jnp.mean(r, axis=-1, keepdims=True)
    factor = lax.rsqrt(jnp.mean(center * center, axis=-1, keepdims=True) + 1e-05)
    return center * factor, factor


def norm_back(normal, factor, dn):
    return factor * (
        dn - jnp.mean(dn, axis=-1, keepdims=True) - normal * jnp.mean(dn * normal, axis=-1, keepdims=True)
    )


def mid_kernel(rchunk, sub, a_ref, x_ref, cot_ref, pad_ref, wout_ref, win_hbm, wback_hbm, b1_ref, pm_ref,
               act_ref, dr1_ref, da_ref, stat_ref, db1_ref,
               win_ref, wback_ref, sem, slope_ref, n1_ref, rs1_ref, low_ref, sum_ref):
    i = pl.program_id(0)
    nchunk, _, width = win_ref.shape
    rows_all = x_ref.shape[0]
    steps = rows_all // rchunk

    def copy_in(j):
        return pltpu.make_async_copy(win_hbm.at[j], win_ref.at[j], sem.at[0, j])

    def copy_back(j):
        return pltpu.make_async_copy(wback_hbm.at[j], wback_ref.at[j], sem.at[1, j])

    @pl.when(i == 0)
    def _():
        for j in range(nchunk):
            copy_in(j).start()
            copy_back(j).start()
        stat_ref[...] = jnp.zeros_like(stat_ref)
        db1_ref[...] = jnp.zeros_like(db1_ref)

    row = lambda n: pm_ref[n : n + 1, :]

    def add_stat(n, v):
        stat_ref[n : n + 1, :] += jnp.sum(v, axis=0, keepdims=True)

    def first(c, t):
        rows = pl.ds(pl.multiple_of(c * rchunk, rchunk), rchunk)
        r = x_ref[rows, :].astype(f32) + dot(a_ref[rows, :], wout_ref[...]) + row(2)
        n1, rs1 = normed(r)
        n1_ref[rows, :] = n1
        rs1_ref[rows, :] = rs1
        low_ref[rows, :] = (n1 * row(3) + row(4)).astype(bf16)
        sum_ref[rows, :] = jnp.zeros_like(n1)
        return t

    lax.fori_loop(0, steps, first, 0)

    def up(j, t):
        @pl.when(i == 0)
        def _():
            copy_in(j).wait()
            copy_back(j).wait()

        for c in range(width // sub):
            cols = slice(c * sub, (c + 1) * sub)
            z = dot(low_ref[...], win_ref[j, :, cols]) + b1_ref[j, :, cols]
            u, slope = gelu_both(z)
            slope_ref[j, :, cols] = slope.astype(bf16)
            sum_ref[...] += dot(u.astype(bf16), wback_ref[j, cols, :])
        return t

    lax.fori_loop(0, nchunk, up, 0)

    def middle(c, t):
        rows = pl.ds(pl.multiple_of(c * rchunk, rchunk), rchunk)
        h1 = n1_ref[rows, :] * row(3) + row(4)
        n2, rs2 = normed(h1 + (sum_ref[rows, :] + row(5)))
        act_ref[rows, :] = n2 * row(6) + row(7)
        dy = cot_ref[rows, :].astype(f32) * pad_ref[rows, :]
        add_stat(6, dy * n2)
        add_stat(7, dy)
        dr2 = norm_back(n2, rs2, dy * row(6))
        add_stat(5, dr2)
        sum_ref[rows, :] = dr2
        low_ref[rows, :] = dr2.astype(bf16)
        return t

    lax.fori_loop(0, steps, middle, 0)

    def down(j, t):
        for c in range(width // sub):
            cols = slice(c * sub, (c + 1) * sub)
            dz = dot(low_ref[...], wback_ref[j, cols, :], NT) * slope_ref[j, :, cols].astype(f32)
            db1_ref[j, :, cols] += jnp.sum(dz, axis=0, keepdims=True)
            sum_ref[...] += dot(dz.astype(bf16), win_ref[j, :, cols], NT)
        return t

    lax.fori_loop(0, nchunk, down, 0)

    def last(c, t):
        rows = pl.ds(pl.multiple_of(c * rchunk, rchunk), rchunk)
        n1 = n1_ref[rows, :]
        dh1 = sum_ref[rows, :]
        add_stat(3, dh1 * n1)
        add_stat(4, dh1)
        dr1 = norm_back(n1, rs1_ref[rows, :], dh1 * row(3))
        add_stat(2, dr1)
        dr1_ref[rows, :] = dr1
        da = dot(dr1.astype(bf16), wout_ref[...], NT).astype(bf16)
        da_ref[rows, :] = da
        add_stat(1, da.astype(f32))
        return t

    lax.fori_loop(0, steps, last, 0)


def mid(a, x, cot, padcol, wout, win_all, wback_all, b1, pm, block=512, rchunk=128, sub=512):
    rows, d = x.shape
    nchunk, _, width = win_all.shape
    block = min(block, rows)
    sub = min(sub, width)
    nb = rows // block
    r = lambda: pl.BlockSpec((block, d), lambda i: (i, 0))
    once = lambda s: pl.BlockSpec(s, lambda i: (0,) * len(s), pipeline_mode=pl.Buffered(1))
    flops = 2 * rows * d * (4 * nchunk * width + 2 * d)
    return pl.pallas_call(
        functools.partial(mid_kernel, rchunk, sub),
        out_shape=(jax.ShapeDtypeStruct((rows, d), f32), jax.ShapeDtypeStruct((rows, d), f32),
                   jax.ShapeDtypeStruct((rows, d), bf16), jax.ShapeDtypeStruct((8, d), f32),
                   jax.ShapeDtypeStruct((nchunk, 1, width), f32)),
        grid_spec=pltpu.PrefetchScalarGridSpec(
            num_scalar_prefetch=0, grid=(nb,),
            in_specs=[r(), r(), r(), pl.BlockSpec((block, 1), lambda i: (i, 0)), once((d, d)),
                      pl.BlockSpec(memory_space=pl.ANY), pl.BlockSpec(memory_space=pl.ANY),
                      once((nchunk, 1, width)), once((8, d))],
            out_specs=[r(), r(), r(), pl.BlockSpec((8, d), lambda i: (0, 0)),
                       pl.BlockSpec((nchunk, 1, width), lambda i: (0, 0, 0))],
            scratch_shapes=[pltpu.VMEM((nchunk, d, width), bf16), pltpu.VMEM((nchunk, width, d), bf16),
                            pltpu.SemaphoreType.DMA((2, nchunk)), pltpu.VMEM((nchunk, block, width), bf16),
                            pltpu.VMEM((block, d), f32), pltpu.VMEM((block, 1), f32),
                            pltpu.VMEM((block, d), bf16), pltpu.VMEM((block, d), f32)]),
        compiler_params=pltpu.CompilerParams(vmem_limit_bytes=60 << 20),
        cost_estimate=pl.CostEstimate(flops=flops, bytes_accessed=40 << 20, transcendentals=2 * rows * nchunk * width),
        name="feed",
    )(a, x, cot, padcol, wout, win_all, wback_all, b1, pm)


def adam_step(grad, first, second, param, average):
    first_new = 0.5 * first + 0.5 * grad
    second_new = 0.5 * second + 0.5 * grad * grad
    corr = 1.0 - 0.5**STEP
    param_new = param - 0.25 * (
        first_new / corr / (jnp.sqrt(second_new / corr) + 1e-08) + 0.01 * param
    )
    return (
        first_new,
        second_new,
        param_new,
        param_new.astype(jnp.bfloat16),
        0.8 * average + 0.2 * param_new,
    )


def on_device(
    tokens,
    segment_ids,
    pad_mask,
    cotangent,
    w_query,
    w_key,
    w_value,
    w_out,
    w_in,
    w_back,
    params_main,
    params_hidden,
    first_main,
    second_main,
    first_hidden,
    second_hidden,
    average_main,
    average_hidden,
):
    rows_all, d = tokens.shape
    width = params_hidden.shape[0]
    total_hidden = width * lax.axis_size("mp")
    seg, pad = segment_ids[0], pad_mask[0]
    in_all = lax.all_gather(w_in, "mp", axis=0, tiled=False)
    back_all = lax.all_gather(w_back, "mp", axis=0, tiled=False)
    bias_all = lax.all_gather(params_hidden, "mp", axis=0, tiled=False)[:, None, :]
    query = (dot(tokens, w_query) + params_main[0]).astype(bf16)
    keys = dot(tokens, w_key).astype(bf16)
    values = (dot(tokens, w_value) + params_main[1]).astype(bf16)
    mixed, lse = attn_fwd(query, keys, values, seg, pad, ALLOWED, 4)
    padcol = pad.astype(f32)[:, None]
    activations, dresid_one, dmixed, stats, hidden_grad = mid(
        mixed, tokens, cotangent, padcol, w_out, in_all, back_all, bias_all, params_main
    )
    dquery, dkeys, dvalues = attn_bwd(query, keys, values, dmixed, lse, seg, pad, ALLOWED, 4)
    input_grad = dresid_one + dot(dquery.astype(bf16), w_query, NT)
    input_grad = input_grad + dot(dkeys.astype(bf16), w_key, NT)
    input_grad = input_grad + dot(dvalues.astype(bf16), w_value, NT)
    local_main = stats.at[0].set(jnp.sum(dquery, axis=0))
    grad_main, hidden_total = lax.psum((local_main, hidden_grad.reshape(total_hidden)), ("dp", "mp"))
    grad_hid = lax.dynamic_slice_in_dim(hidden_total, lax.axis_index("mp") * width, width, 0)
    grad_norm = jnp.sqrt(jnp.sum(grad_main * grad_main) + jnp.sum(hidden_total * hidden_total))
    tokens_all = rows_all * lax.axis_size("dp") * lax.axis_size("mp")
    limit = 0.01 * math.sqrt(tokens_all * (8 * d + total_hidden))
    scale_factor = jnp.minimum(1.0, limit / (grad_norm + 1e-06))
    grad_main = grad_main * scale_factor
    grad_hid = grad_hid * scale_factor
    fm, sm, pm, cm, am = adam_step(grad_main, first_main, second_main, params_main, average_main)
    fh, sh, ph, ch, ah = adam_step(grad_hid, first_hidden, second_hidden, params_hidden, average_hidden)
    return (
        activations,
        input_grad,
        grad_norm,
        grad_main,
        grad_hid,
        fm,
        sm,
        fh,
        sh,
        pm,
        ph,
        cm,
        ch,
        am,
        ah,
    )


def solution(mesh):
    placed = (
        P(("dp", "mp"), None),
        P(("dp", "mp"), None),
        P(("dp", "mp"), None),
        P(("dp", "mp"), None),
        P(),
        P(),
        P(),
        P(),
        P(None, "mp"),
        P("mp", None),
        P(),
        P("mp"),
        P(),
        P(),
        P("mp"),
        P("mp"),
        P(),
        P("mp"),
    )
    return jax.shard_map(
        on_device,
        mesh=mesh,
        in_specs=placed,
        out_specs=(
            P(("dp", "mp"), None),
            P(("dp", "mp"), None),
            P(),
            P(),
            P("mp"),
            P(),
            P(),
            P("mp"),
            P("mp"),
            P(),
            P("mp"),
            P(),
            P("mp"),
            P(),
            P("mp"),
        ),
        check_vma=False,
    )
```

time: 640 us -> 325 us (0.51)
  matrix products: 379 us -> 23.6 us
  Pallas kernels: 0 us -> 167 us
  other arithmetic: 117 us -> 6.7 us
  local copies, waits for them, and re-layouts: 61.6 us -> 6.81 us
  waiting for transfers between devices: 1.38 us -> 50.4 us
  loops' own time: 11.5 us -> 0 us
    dot_general x26 -> x6, matrix products: 379 us -> 23.6 us  [dot(): return lax.dot_general(a, b, dims, preferred_element_type=f32)]
    pallas_call x0 -> x3, Pallas kernels: none -> 167 us  [the longest x1 77.1 us: mid(): pl.pallas_call(functools.partial(mid_kernel, rchunk, sub), out_shape=(jax...]
    convert_element_type x4 -> x1, other arithmetic: 58.8 us -> 0.01 us  [on_device(): padcol = pad.astype(f32)[:, None]]
    all_gather x1, waiting for transfers between devices: 0.01 us -> 49 us  [on_device(): back_all = lax.all_gather(w_back, 'mp', axis=0, tiled=False)]
    reduce_sum x9 -> x3, other arithmetic: 47.9 us -> 2.91 us  [the longest x1 2.5 us: on_device(): local_main = stats.at[0].set(jnp.sum(dquery, axis=0))]
    unnamed x120 -> x56, local copies, waits for them, and re-layouts: 36.7 us -> 3.8 us
    squeeze x2 -> x0, local copies, waits for them, and re-layouts: 12.7 us -> none  [on_device(): lax.map(attend_seq, (q_blocks, k_seqs, v_seqs, segment_ids, pad_mask))]
    another operation x2 -> x0, loops' own time: 11.5 us -> none  [the longest x1 5.81 us: back_seq(): lax.scan(one_step, (empty, empty), jnp.arange(nblock))]
  transfers between devices with their start and end apart: 2 -> 2, of which waited for: 0 -> 1; matrix products, arithmetic and copies ran while one was open for 30% -> 5% of each run, Pallas kernels for 0% -> 11%
where the time goes in v2:
time: 325 us; the launch traced here: 326 us
  Pallas kernels  167 us (51%)
  blocking collectives  53.5 us (16%)
  waiting for transfers between devices  50.4 us (16%)
  matrix products  23.6 us (7%)
  between operations  17.2 us (5%)
  local copies, waits for them, and re-layouts  6.81 us (2%)
  other arithmetic  6.7 us (2%)
    pallas_call x1, Pallas kernels, mid(): pl.pallas_call(functools.partial(mid_kernel, rchunk, sub), out_shape=(jax...  77.1 us
    pallas_call x1, Pallas kernels, attn_bwd(): pl.pallas_call(functools.partial(bwd_kernel, allowed, npair, unroll), out...  53.8 us
    all_gather x1, waiting for transfers between devices, on_device(): back_all = lax.all_gather(w_back, 'mp', axis=0, tiled=False)  49 us
    psum x1, blocking collectives, on_device(): lax.psum((local_main, hidden_grad.reshape(total_hidden)), ('dp', 'mp'))  42 us
    pallas_call x1, Pallas kernels, attn_fwd(): pl.pallas_call(functools.partial(fwd_kernel, allowed, npair, unroll), out...  36.6 us
    dot_general x6, matrix products, dot(): return lax.dot_general(a, b, dims, preferred_element_type=f32)  23.6 us
    all_gather x1, blocking collectives, on_device(): lax.all_gather(params_hidden, 'mp', axis=0, tiled=False)[:, None, :]  11.5 us
  transfers between devices with their start and end apart: 2, of which 1 were waited for; matrix products, arithmetic and copies ran while one was open for 5% of the time, Pallas kernels for 11%

profile of v2, /device:TPU:0, one launch (start us, length us, event | category | flops | bytes accessed | tf_op | source)
XLA Modules:
  0.0 325.7 jit_solution(15656542374579795537)
XLA Ops:
  7.3 0.7 all-gather.7.cloned.1.call-update
  8.0 0.7 all-gather.9.cloned.1.call-update
  8.9 0.2 convert_reduce_fusion
  9.2 0.2 convert_reduce_fusion.2
  9.4 0.6 gather_fusion
  10.0 0.2 copy.41.segcol_ref
  10.3 1.0 copy.42.pad_ref
  11.3 0.8 fusion.15
  12.2 6.0 %convolution_convert_fusion.k_ref = bf16[1024,1024]{1,0:T(8,128)(2,1)} fusion(bf16[1024,1024]{1,0:T(8,128)(2,1)} %x_ref.1, bf16[1024,1024]{1,0:T(8,128)(2,1)} %param.27), kind=kOutput, calls=%fused_computation.10 | convolution fusion | flops 2148532224 | bytes 6291456 | tf_op jit(solution)/shard_map/dot_general | solution.py:188
  18.2 3.6 %add_convert_fusion.v_ref = bf16[1024,1024]{1,0:T(8,128)(2,1)} fusion(f32[1024]{0:T(1024)S(1)} %bitcast.45, bf16[1024,1024]{1,0:T(8,128)(2,1)S(1)} %copy-done.26, bf16[1024,1024]{1,0:T(8,128)(2,1)S(1)} %copy-done), kind=kOutput, calls=%fused_computation.2 | convolution fusion | flops 2149580800 | bytes 6295552 | tf_op jit(solution)/shard_map/dot_general | solution.py:188
  21.9 2.4 add_convert_fusion.1.q_ref
  24.3 36.6 %attend.1 = (bf16[1024,1024]{1,0:T(8,128)(2,1)S(1)}, f32[8,8,256]{2,1,0:T(8,128)S(1)}) custom-call(s32[2,8]{1,0:T(2,128)S(1)} %pad_add_fusion.win_ref, bf16[1024,1024]{1,0:T(8,128)(2,1)S(1)} %add_convert_fusion.1.q_ref, bf16[1024,1024]{1,0:T(8,128)(2,1)} %convolution_convert_fusion.k_ref, bf16[1024,1024]{1,0:T(8,128)(2,1)} %add_convert_fusion.v_ref, ...), custom_call_target="tpu_custom_call" | custom-call | tf_op jit(solution)/shard_map/attend/pallas_call | solution.py:104
  60.9 0.6 copy-done.3
  61.5 1.4 copy-done.6
  62.9 11.5 %all-gather.3.b1_ref = f32[8,1,512]{2,1,0:T(1,128)} all-gather(f32[1,1,512]{2,1,0:T(1,128)S(1)} %bitcast.43), channel_id=4, replica_groups=mesh['dp'=4,'mp'=8] {'mp'}, dimensions={0}, use_global_device_ids=true | all-gather | bytes 18432 | tf_op jit(solution)/shard_map/all_gather | solution.py:384
  74.4 49.0 %all-gather.9.cloned.1.call-done = bf16[4096,1024]{1,0:T(8,128)(2,1)} async-done(((bf16[512,1024]{1,0:T(8,128)(2,1)}), bf16[4096,1024]{1,0:T(8,128)(2,1)}) %all-gather.9.cloned.1.call-update) | async-done | bytes 8388624 | tf_op jit(solution)/shard_map/all_gather | solution.py:383
  123.4 77.1 %feed.1 = (f32[1024,1024]{1,0:T(8,128)}, f32[1024,1024]{1,0:T(8,128)}, bf16[1024,1024]{1,0:T(8,128)(2,1)}, f32[8,1024]{1,0:T(8,128)}, f32[8,1,512]{2,1,0:T(1,128)}) custom-call(bf16[1024,1024]{1,0:T(8,128)(2,1)} %copy-done.6, bf16[1024,1024]{1,0:T(8,128)(2,1)} %x_ref.1, bf16[1024,1024]{1,0:T(8,128)(2,1)} %cot_ref.1, f32[1024,1]{1,0:T(8,128)} %copy.42.pad_ref, ...), custom_call_target="tpu_custom_call" | custom-call | flops 38654705664 | bytes 41943040 | tf_op jit(solution)/shard_map/feed/pallas_call | solution.py:320
  200.5 53.8 %attend_back.1 = (f32[1024,1024]{1,0:T(8,128)}, f32[1024,1024]{1,0:T(8,128)}, f32[1024,1024]{1,0:T(8,128)}) custom-call(s32[2,8]{1,0:T(2,128)} %copy-done.5, bf16[1024,1024]{1,0:T(8,128)(2,1)} %copy-done.1, bf16[1024,1024]{1,0:T(8,128)(2,1)} %convolution_convert_fusion.k_ref, bf16[1024,1024]{1,0:T(8,128)(2,1)} %add_convert_fusion.v_ref, ...), custom_call_target="tpu_custom_call" | custom-call | tf_op jit(solution)/shard_map/attend_back/pallas_call | solution.py:173
  254.4 2.5 reduce_sum.84
  256.9 0.1 scatter.4
  257.0 42.0 %all-reduce = (f32[8,1024]{1,0:T(8,128)S(1)}, f32[4096]{0:T(1024)S(1)}) all-reduce(f32[8,1024]{1,0:T(8,128)S(1)} %scatter.4, f32[4096]{0:T(1024)S(1)} %bitcast.42), channel_id=1, replica_groups=mesh['dp'=4,'mp'=8] {'dp','mp'}, use_global_device_ids=true, to_apply=%region_5.6 | all-reduce | flops 12288 | bytes 98304 | tf_op jit(solution)/shard_map/psum | solution.py:398
  299.0 0.6 multiply_reduce_fusion
  299.7 0.6 multiply_reduce_fusion.1
  301.7 0.7 multiply_add_fusion.1
  302.3 0.6 convert_element_type.63
  303.0 0.7 multiply_add_fusion.3
  303.6 0.6 convert_element_type.64
  304.2 4.7 %fusion = f32[1024,1024]{1,0:T(8,128)S(1)} fusion(bf16[1024,1024]{1,0:T(8,128)(2,1)S(1)} %copy-done, f32[1024,1024]{1,0:T(8,128)} %get-tuple-element.44), kind=kOutput, calls=%fused_computation.4 | convolution fusion | flops 2148532224 | bytes 10485760 | tf_op jit(solution)/shard_map/dot_general | solution.py:188
  309.0 2.4 fusion.2
  311.4 1.0 copy-done.9
  312.4 0.6 copy-done.11
  313.0 4.5 %add_add_fusion = f32[1024,1024]{1,0:T(8,128)} fusion(f32[1024,1024]{1,0:T(8,128)S(1)} %fusion, f32[1024,1024]{1,0:T(8,128)S(1)} %fusion.2, f32[1024,1024]{1,0:T(8,128)S(1)} %copy-done.9, bf16[1024,1024]{1,0:T(8,128)(2,1)S(1)} %copy-done.11, f32[1024,1024]{1,0:T(8,128)S(1)} %copy-done.8), kind=kOutput, calls=%fused_computation.1 | convolution fusion | flops 2151677952 | bytes 23068672 | tf_op jit(solution)/shard_map/dot_general | solution.py:188
  (63 shorter events, 0.5 us)
Async XLA Ops:
  7.2 11.0 %copy-start = (bf16[1024,1024]{1,0:T(8,128)(2,1)S(1)}, bf16[1024,1024]{1,0:T(8,128)(2,1)}, u32[]{:S(2)}) copy-start(bf16[1024,1024]{1,0:T(8,128)(2,1)} %param.28) | copy-start | bytes 6291460
  7.2 2.0 copy-start.7
  7.2 1.5 copy-start.4
  7.2 2.8 copy-start.21
  7.2 67.2 %all-gather.7.cloned.1.call-start = ((), (), s32[]{:S(2)}) async-start(), calls=%async_computation | async-start | bytes 9437184 | tf_op jit(solution)/shard_map/all_gather | solution.py:382
  8.0 115.4 %all-gather.9.cloned.1.call-start = ((), (), s32[]{:S(2)}) async-start(), calls=%async_computation.1 | async-start | bytes 9437184 | tf_op jit(solution)/shard_map/all_gather | solution.py:383
  10.3 14.0 %copy-start.2 = (s32[1024,1]{1,0:T(8,128)}, s32[1024,1]{1,0:T(8,128)S(1)}, u32[]{:S(2)}) copy-start(s32[1024,1]{1,0:T(8,128)S(1)} %copy.41.segcol_ref) | copy-start | bytes 12292
  11.3 12.9 %copy-start.5 = (s32[2,8]{1,0:T(2,128)}, s32[2,8]{1,0:T(2,128)S(1)}, u32[]{:S(2)}) copy-start(s32[2,8]{1,0:T(2,128)S(1)} %pad_add_fusion.win_ref) | copy-start | bytes 196
  12.2 6.0 %copy-start.26 = (bf16[1024,1024]{1,0:T(8,128)(2,1)S(1)}, bf16[1024,1024]{1,0:T(8,128)(2,1)}, u32[]{:S(2)}) copy-start(bf16[1024,1024]{1,0:T(8,128)(2,1)} %x_ref.1) | copy-start | bytes 6291460
  18.2 3.6 %copy-start.10 = (bf16[1024,1024]{1,0:T(8,128)(2,1)S(1)}, bf16[1024,1024]{1,0:T(8,128)(2,1)}, u32[]{:S(2)}) copy-start(bf16[1024,1024]{1,0:T(8,128)(2,1)} %param.26) | copy-start | bytes 6291460
  24.3 36.6 %copy-start.1 = (bf16[1024,1024]{1,0:T(8,128)(2,1)}, bf16[1024,1024]{1,0:T(8,128)(2,1)S(1)}, u32[]{:S(2)}) copy-start(bf16[1024,1024]{1,0:T(8,128)(2,1)S(1)} %add_convert_fusion.1.q_ref) | copy-start | bytes 6291460
  24.3 38.6 %copy-start.19 = (f32[512]{0:T(512)S(1)}, f32[512]{0:T(512)}, u32[]{:S(2)}) copy-start(f32[512]{0:T(512)} %param.33) | copy-start | bytes 6148
  60.9 0.6 copy-start.3
  61.5 1.4 copy-start.6
  254.3 2.6 copy-start.17
  254.3 2.7 copy-start.18
  254.3 47.3 %copy-start.13 = (f32[8,1024]{1,0:T(8,128)S(1)}, f32[8,1024]{1,0:T(8,128)}, u32[]{:S(2)}) copy-start(f32[8,1024]{1,0:T(8,128)} %pm_ref.1) | copy-start | bytes 98308
  254.3 47.3 %copy-start.14 = (f32[8,1024]{1,0:T(8,128)S(1)}, f32[8,1024]{1,0:T(8,128)}, u32[]{:S(2)}) copy-start(f32[8,1024]{1,0:T(8,128)} %param.38) | copy-start | bytes 98308
  254.4 47.3 %copy-start.15 = (f32[8,1024]{1,0:T(8,128)S(1)}, f32[8,1024]{1,0:T(8,128)}, u32[]{:S(2)}) copy-start(f32[8,1024]{1,0:T(8,128)} %param.35) | copy-start | bytes 98308
  254.4 47.3 %copy-start.16 = (f32[8,1024]{1,0:T(8,128)S(1)}, f32[8,1024]{1,0:T(8,128)}, u32[]{:S(2)}) copy-start(f32[8,1024]{1,0:T(8,128)} %param.34) | copy-start | bytes 98308
  254.4 48.6 %copy-start.22 = (f32[512]{0:T(512)S(1)}, f32[512]{0:T(512)}, u32[]{:S(2)}) copy-start(f32[512]{0:T(512)} %param.39) | copy-start | bytes 6148
  254.4 48.6 %copy-start.23 = (f32[512]{0:T(512)S(1)}, f32[512]{0:T(512)}, u32[]{:S(2)}) copy-start(f32[512]{0:T(512)} %param.37) | copy-start | bytes 6148
  254.4 48.6 %copy-start.24 = (f32[512]{0:T(512)S(1)}, f32[512]{0:T(512)}, u32[]{:S(2)}) copy-start(f32[512]{0:T(512)} %param.36) | copy-start | bytes 6148
  302.3 6.6 %copy-start.12 = (f32[8,1024]{1,0:T(8,128)}, f32[8,1024]{1,0:T(8,128)S(1)}, u32[]{:S(2)}) copy-start(f32[8,1024]{1,0:T(8,128)S(1)} %get-tuple-element.57) | copy-start | bytes 98308
  303.6 5.3 %copy-start.20 = (f32[512]{0:T(512)}, f32[512]{0:T(512)S(1)}, u32[]{:S(2)}) copy-start(f32[512]{0:T(512)S(1)} %get-tuple-element.52) | copy-start | bytes 6148
  304.2 4.7 %copy-start.25 = (f32[1024,1024]{1,0:T(8,128)S(1)}, f32[1024,1024]{1,0:T(8,128)}, u32[]{:S(2)}) copy-start(f32[1024,1024]{1,0:T(8,128)} %get-tuple-element.43) | copy-start | bytes 12582916
  304.2 4.7 %copy-start.27 = (bf16[1024,1024]{1,0:T(8,128)(2,1)S(1)}, bf16[1024,1024]{1,0:T(8,128)(2,1)}, u32[]{:S(2)}) copy-start(bf16[1024,1024]{1,0:T(8,128)(2,1)} %param.27) | copy-start | bytes 6291460
  309.0 2.4 copy-start.8
  309.0 3.5 %copy-start.9 = (f32[1024,1024]{1,0:T(8,128)S(1)}, f32[1024,1024]{1,0:T(8,128)}, u32[]{:S(2)}) copy-start(f32[1024,1024]{1,0:T(8,128)} %get-tuple-element.39) | copy-start | bytes 12582916
  309.0 4.0 %copy-start.11 = (bf16[1024,1024]{1,0:T(8,128)(2,1)S(1)}, bf16[1024,1024]{1,0:T(8,128)(2,1)}, u32[]{:S(2)}) copy-start(bf16[1024,1024]{1,0:T(8,128)(2,1)} %param.26) | copy-start | bytes 6291460
Sparse Core Ops, SparseCore 0:
  10.0 57.0 all-gather.6
  69.0 54.3 all-gather.8
